TPU v7x, 256 devices: a whole 4x4x8 slice. The times are simulated.
256 devices in a mesh: blk: 16 (over y, x_lo, core), inner: 16 (over x_hi, z).
Axes of the slice: x: 4 (x_hi: 2, x_lo: 2; x = x_hi * 2 + x_lo), y: 4, z: 8, core: 2. Of those that a mesh axis runs over, the one named last changes fastest.
Arguments:
- records: float32 [2048, 64, 2048], P('blk', 'inner'), may hold values from -6 to 6
- starts: int32 [64], P('inner'), may hold values from 0 to 1024, as said below
- offsets: int32 [2048, 16], P('blk'), may hold values from -256 to 256, as said below
Outputs:
- correlations: float32 [16, 2048, 768], P('inner', 'blk')
Inputs may be any that keep to these rules, and one draw needn't show every extreme that they name: Segment s uses samples starts[s] to starts[s] + 1023 of its slot. `offsets`: never zero; the partner of channel c is (c + offset) mod 2048.
All inputs are finite; a program needn't handle non-finite values.
Results may differ from a plain program's by a relative error of at most 0.0003.
Values sent between devices are 32-bit elements; how exact they have to be, the bound alone decides.
A program may use at most 128 MiB of HBM per device.

v0:
```python
import math

import jax
import jax.numpy as jnp
from jax import lax
from jax.sharding import PartitionSpec as P

SEG = 1024
LAGS = 768
HALF = 32
PAIRS = 16
F = 512


def shifted(value, axis, steps):
    count = lax.axis_size(axis)
    pairs = [(source, (source + steps) % count) for source in range(count)]
    return lax.ppermute(value, axis, pairs)


def cut_segment(slot_rows, begin):
    return lax.dynamic_slice_in_dim(slot_rows, begin, SEG, 1)


def lag_rows(bin_ids, half_ids, factor):
    shifts = jnp.arange(LAGS, dtype=jnp.int32) - LAGS // 2
    phase = bin_ids[:, None] * shifts[None, :] % SEG
    angle = 2.0 * jnp.pi / SEG * phase.astype(jnp.float32)
    table = jnp.where(half_ids[:, None] == 0, jnp.cos(angle), -jnp.sin(angle))
    return table * factor


def local(records, starts, offsets):
    channels_here = records.shape[0]
    groups = lax.axis_size("inner")
    group_index = lax.axis_index("inner")
    width = F // groups
    samples = jnp.arange(SEG, dtype=jnp.int32)
    window = 0.5 - 0.5 * jnp.cos(2.0 * jnp.pi * samples.astype(jnp.float32) / SEG)
    pieces = jax.vmap(cut_segment, in_axes=(1, 0), out_axes=1)(records, starts) * window
    segment_rows = pieces.reshape(-1, SEG)
    columns = jnp.arange(2 * F, dtype=jnp.int32)
    column_half = columns // width % 2
    column_bin = columns // (2 * width) * width + columns % width
    phase = samples[:, None] * column_bin[None, :] % SEG
    angle = 2.0 * jnp.pi / SEG * phase.astype(jnp.float32)
    forward = jnp.where(column_half[None, :] == 0, jnp.cos(angle), -jnp.sin(angle))
    spectra = jnp.dot(
        segment_rows, forward, precision=lax.Precision.HIGHEST, preferred_element_type=jnp.float32
    )
    split_spectra = spectra.reshape(-1, groups, 2, width)
    real_part = split_spectra[:, :, 0, :].reshape(-1, F)
    imag_part = split_spectra[:, :, 1, :].reshape(-1, F)
    bins = jnp.arange(F, dtype=jnp.int32)
    distance = jnp.abs(bins[:, None] - bins[None, :])
    distance = jnp.minimum(distance, F - distance)
    band = (distance <= HALF).astype(jnp.float32) / (2 * HALF + 1)
    power = real_part * real_part + imag_part * imag_part
    smooth = jnp.dot(
        power, band, precision=lax.Precision.HIGHEST, preferred_element_type=jnp.float32
    )
    scale = lax.rsqrt(smooth + 1e-06)
    whitened = (split_spectra * scale.reshape(-1, groups, 1, width)).reshape(
        channels_here, -1, 2 * F
    )
    owned = lax.all_to_all(whitened, "inner", split_axis=2, concat_axis=1, tiled=True)
    segment_count = owned.shape[1]
    flat_owned = owned.reshape(channels_here, -1)
    lower_blocks = []
    current = flat_owned
    for hop_number in range(2):
        current = shifted(current, "blk", 1)
        lower_blocks.append(current)
    upper_blocks = []
    current = flat_owned
    for hop_number in range(2):
        current = shifted(current, "blk", -1)
        upper_blocks.append(current)
    extended = jnp.concatenate(
        [lower_blocks[1], lower_blocks[0], flat_owned, upper_blocks[0], upper_blocks[1]], 0
    )
    extended = extended.reshape(5 * channels_here, segment_count, 2, width)
    own_spectra = owned.reshape(channels_here, segment_count, 2, width)
    own_re = own_spectra[:, :, 0, :]
    own_im = own_spectra[:, :, 1, :]
    local_ids = jnp.arange(channels_here, dtype=jnp.int32) + 2 * channels_here
    factor = math.sqrt(segment_count / F)
    local_rows = jnp.arange(2 * width, dtype=jnp.int32)
    local_table = lag_rows(group_index * width + local_rows % width, local_rows // width, factor)

    def one_pair(column_offsets):
        partner = extended[local_ids + column_offsets]
        partner_re = partner[:, :, 0, :]
        partner_im = partner[:, :, 1, :]
        cross_re = jnp.sum(own_re * partner_re + own_im * partner_im, axis=1) / segment_count
        cross_im = jnp.sum(own_im * partner_re - own_re * partner_im, axis=1) / segment_count
        return jnp.concatenate([cross_re, cross_im], 1)

    cross = lax.map(one_pair, offsets.T)
    joined = cross.reshape(lax.axis_size("inner") * (PAIRS // groups) * channels_here, 2 * width)
    result = jnp.dot(
        joined, local_table, precision=lax.Precision.HIGHEST, preferred_element_type=jnp.float32
    )
    return lax.psum_scatter(
        result.reshape(lax.axis_size("inner") * (PAIRS // groups), channels_here, LAGS),
        "inner",
        scatter_dimension=0,
        tiled=True,
    )


def solution(mesh):
    placed = (P("blk", "inner", None), P("inner"), P("blk", None))
    return jax.shard_map(
        local, mesh=mesh, in_specs=placed, out_specs=P("inner", "blk", None), check_vma=False
    )
```

profile of v0, /device:TPU:1, one launch (start us, length us, event | category | flops | bytes accessed | tf_op | source)
XLA Modules:
  0.0 737.9 jit_solution(15963438975208695441)
XLA Ops:
  6.7 6.6 copy.60
  13.4 12.7 %while.12 = (s32[]{:T(128)}, f32[4,128,2048]{2,1,0:T(8,128)}, s32[4,3]{1,0:T(4,128)S(1)}, f32[4,128,1024]{2,1,0:T(8,128)S(1)}, s32[]{:T(128)}) while((s32[]{:T(128)}, f32[4,128,2048]{2,1,0:T(8,128)}, s32[4,3]{1,0:T(4,128)S(1)}, f32[4,128,1024]{2,1,0:T(8,128)S(1)}, s32[]{:T(128)}) %tuple.60), condition=%wide.while_cond, body=%wide.while_body.sunk | while | flops 2 | bytes 1048693 | solution.py:22
  29.5 26.0 %fusion.7 = f32[512,16,2,32]{0,3,2,1:T(8,128)S(1)} fusion(f32[512,1024,1,1]{1,0,2,3:T(8,128)} %reshape.238, s32[16,2,32]{2,1,0:T(2,128)S(1)} %fusion.58, pred[16,2,32]{2,1,0:T(4,128)(4,1)S(1)} %fusion.60), kind=kOutput, calls=%fused_computation.22 | convolution fusion | flops 6459228160 | bytes 4199424 | tf_op jit(solution)/shard_map/dot_general | solution.py:48
  58.2 8.8 %copy.47 = f32[512,16,2,32]{3,2,1,0:T(2,128)} copy(f32[512,16,2,32]{0,3,2,1:T(8,128)S(1)} %broadcast_multiply_fusion.2) | data formatting | bytes 4194304 | tf_op jit(solution)/shard_map/mul | solution.py:63
  67.0 9.5 %reshape.201 = f32[128,4,1024]{2,1,0:T(4,128)S(1)} reshape(f32[512,16,2,32]{3,2,1,0:T(2,128)} %copy.47) | data formatting | bytes 4194304 | tf_op jit(solution)/shard_map/reshape | solution.py:63
  79.1 60.5 %all_to_all.15 = f32[128,4,1024]{0,1,2:T(4,128)S(1)} all-to-all(f32[128,4,1024]{0,1,2:T(4,128)} %copy.48), channel_id=1, replica_groups=mesh['blk'=16,'inner'=16] {'inner'}, dimensions={2} | all-to-all | bytes 4194304 | tf_op jit(solution)/shard_map/all_to_all | solution.py:66
  143.2 41.5 %collective-permute-done = f32[128,4096]{0,1:T(8,128)} collective-permute-done((f32[128,4096]{0,1:T(8,128)S(1)}, f32[128,4096]{0,1:T(8,128)}, u32[]{:S(2)}, u32[]{:S(2)}) %collective-permute-start) | collective-permute-done | bytes 2097184 | tf_op jit(solution)/shard_map/ppermute | solution.py:18
  187.3 4.1 collective-permute-done.2
  199.3 26.1 %collective-permute-done.1 = f32[128,4096]{0,1:T(8,128)} collective-permute-done((f32[128,4096]{0,1:T(8,128)}, f32[128,4096]{0,1:T(8,128)}, u32[]{:S(2)}, u32[]{:S(2)}) %collective-permute-start.1) | collective-permute-done | bytes 2097184 | tf_op jit(solution)/shard_map/ppermute | solution.py:18
  243.0 20.2 %copy.52 = f32[640,64,2,32]{1,3,2,0:T(8,128)} copy(f32[640,64,2,32]{0,3,2,1:T(8,128)} %constant_dynamic-update-slice_fusion) | data formatting | bytes 20971520
  263.2 234.3 %while.13 = (s32[]{:T(128)}, f32[16,128,64]{2,1,0:T(8,128)S(1)}, s32[16,128]{1,0:T(8,128)}, f32[640,64,2,32]{1,3,2,0:T(8,128)}, f32[128,64,32]{1,2,0:T(8,128)S(1)}, /*index=5*/f32[128,64,32]{1,2,0:T(8,128)}, s32[]{:T(128)}) while((s32[]{:T(128)}, f32[16,128,64]{2,1,0:T(8,128)S(1)}, s32[16,128]{1,0:T(8,128)}, ...), condition=%wide.region_3.4_spmd.clone, body=%wide.region_0.3_spmd.clone.sunk | while | flops 2107010 | bytes 8689749 | solution.py:99
  263.9 9.8 %gather_fusion = f32[128,64,2,32]{1,3,2,0:T(8,128)} fusion(f32[640,64,2,32]{1,3,2,0:T(8,128)} %get-tuple-element.249, s32[1024]{0:T(1024)S(1)} %pad_clamp_fusion.2), kind=kCustom, calls=%fused_computation.clone.clone.1 | custom fusion | bytes 4194816 | tf_op jit(solution)/shard_map/while/body/eval_jaxpr/gather | solution.py:92
  278.6 9.8 %gather_fusion = f32[128,64,2,32]{1,3,2,0:T(8,128)} fusion(f32[640,64,2,32]{1,3,2,0:T(8,128)} %get-tuple-element.249, s32[1024]{0:T(1024)S(1)} %pad_clamp_fusion.2), kind=kCustom, calls=%fused_computation.clone.clone.1 | custom fusion | bytes 4194816 | tf_op jit(solution)/shard_map/while/body/eval_jaxpr/gather | solution.py:92
  288.3 4.1 add_reduce_fusion.2
  293.2 9.8 %gather_fusion = f32[128,64,2,32]{1,3,2,0:T(8,128)} fusion(f32[640,64,2,32]{1,3,2,0:T(8,128)} %get-tuple-element.249, s32[1024]{0:T(1024)S(1)} %pad_clamp_fusion.2), kind=kCustom, calls=%fused_computation.clone.clone.1 | custom fusion | bytes 4194816 | tf_op jit(solution)/shard_map/while/body/eval_jaxpr/gather | solution.py:92
  303.0 4.1 add_reduce_fusion.2
  307.9 9.8 %gather_fusion = f32[128,64,2,32]{1,3,2,0:T(8,128)} fusion(f32[640,64,2,32]{1,3,2,0:T(8,128)} %get-tuple-element.249, s32[1024]{0:T(1024)S(1)} %pad_clamp_fusion.2), kind=kCustom, calls=%fused_computation.clone.clone.1 | custom fusion | bytes 4194816 | tf_op jit(solution)/shard_map/while/body/eval_jaxpr/gather | solution.py:92
  317.6 4.1 add_reduce_fusion.2
  322.5 9.8 %gather_fusion = f32[128,64,2,32]{1,3,2,0:T(8,128)} fusion(f32[640,64,2,32]{1,3,2,0:T(8,128)} %get-tuple-element.249, s32[1024]{0:T(1024)S(1)} %pad_clamp_fusion.2), kind=kCustom, calls=%fused_computation.clone.clone.1 | custom fusion | bytes 4194816 | tf_op jit(solution)/shard_map/while/body/eval_jaxpr/gather | solution.py:92
  337.1 9.8 %gather_fusion = f32[128,64,2,32]{1,3,2,0:T(8,128)} fusion(f32[640,64,2,32]{1,3,2,0:T(8,128)} %get-tuple-element.249, s32[1024]{0:T(1024)S(1)} %pad_clamp_fusion.2), kind=kCustom, calls=%fused_computation.clone.clone.1 | custom fusion | bytes 4194816 | tf_op jit(solution)/shard_map/while/body/eval_jaxpr/gather | solution.py:92
  351.8 9.8 %gather_fusion = f32[128,64,2,32]{1,3,2,0:T(8,128)} fusion(f32[640,64,2,32]{1,3,2,0:T(8,128)} %get-tuple-element.249, s32[1024]{0:T(1024)S(1)} %pad_clamp_fusion.2), kind=kCustom, calls=%fused_computation.clone.clone.1 | custom fusion | bytes 4194816 | tf_op jit(solution)/shard_map/while/body/eval_jaxpr/gather | solution.py:92
  366.4 9.8 %gather_fusion = f32[128,64,2,32]{1,3,2,0:T(8,128)} fusion(f32[640,64,2,32]{1,3,2,0:T(8,128)} %get-tuple-element.249, s32[1024]{0:T(1024)S(1)} %pad_clamp_fusion.2), kind=kCustom, calls=%fused_computation.clone.clone.1 | custom fusion | bytes 4194816 | tf_op jit(solution)/shard_map/while/body/eval_jaxpr/gather | solution.py:92
  381.1 9.8 %gather_fusion = f32[128,64,2,32]{1,3,2,0:T(8,128)} fusion(f32[640,64,2,32]{1,3,2,0:T(8,128)} %get-tuple-element.249, s32[1024]{0:T(1024)S(1)} %pad_clamp_fusion.2), kind=kCustom, calls=%fused_computation.clone.clone.1 | custom fusion | bytes 4194816 | tf_op jit(solution)/shard_map/while/body/eval_jaxpr/gather | solution.py:92
  395.7 9.8 %gather_fusion = f32[128,64,2,32]{1,3,2,0:T(8,128)} fusion(f32[640,64,2,32]{1,3,2,0:T(8,128)} %get-tuple-element.249, s32[1024]{0:T(1024)S(1)} %pad_clamp_fusion.2), kind=kCustom, calls=%fused_computation.clone.clone.1 | custom fusion | bytes 4194816 | tf_op jit(solution)/shard_map/while/body/eval_jaxpr/gather | solution.py:92
  410.4 9.8 %gather_fusion = f32[128,64,2,32]{1,3,2,0:T(8,128)} fusion(f32[640,64,2,32]{1,3,2,0:T(8,128)} %get-tuple-element.249, s32[1024]{0:T(1024)S(1)} %pad_clamp_fusion.2), kind=kCustom, calls=%fused_computation.clone.clone.1 | custom fusion | bytes 4194816 | tf_op jit(solution)/shard_map/while/body/eval_jaxpr/gather | solution.py:92
  425.0 9.8 %gather_fusion = f32[128,64,2,32]{1,3,2,0:T(8,128)} fusion(f32[640,64,2,32]{1,3,2,0:T(8,128)} %get-tuple-element.249, s32[1024]{0:T(1024)S(1)} %pad_clamp_fusion.2), kind=kCustom, calls=%fused_computation.clone.clone.1 | custom fusion | bytes 4194816 | tf_op jit(solution)/shard_map/while/body/eval_jaxpr/gather | solution.py:92
  439.7 9.8 %gather_fusion = f32[128,64,2,32]{1,3,2,0:T(8,128)} fusion(f32[640,64,2,32]{1,3,2,0:T(8,128)} %get-tuple-element.249, s32[1024]{0:T(1024)S(1)} %pad_clamp_fusion.2), kind=kCustom, calls=%fused_computation.clone.clone.1 | custom fusion | bytes 4194816 | tf_op jit(solution)/shard_map/while/body/eval_jaxpr/gather | solution.py:92
  454.3 9.8 %gather_fusion = f32[128,64,2,32]{1,3,2,0:T(8,128)} fusion(f32[640,64,2,32]{1,3,2,0:T(8,128)} %get-tuple-element.249, s32[1024]{0:T(1024)S(1)} %pad_clamp_fusion.2), kind=kCustom, calls=%fused_computation.clone.clone.1 | custom fusion | bytes 4194816 | tf_op jit(solution)/shard_map/while/body/eval_jaxpr/gather | solution.py:92
  468.9 9.8 %gather_fusion = f32[128,64,2,32]{1,3,2,0:T(8,128)} fusion(f32[640,64,2,32]{1,3,2,0:T(8,128)} %get-tuple-element.249, s32[1024]{0:T(1024)S(1)} %pad_clamp_fusion.2), kind=kCustom, calls=%fused_computation.clone.clone.1 | custom fusion | bytes 4194816 | tf_op jit(solution)/shard_map/while/body/eval_jaxpr/gather | solution.py:92
  483.6 9.8 %gather_fusion = f32[128,64,2,32]{1,3,2,0:T(8,128)} fusion(f32[640,64,2,32]{1,3,2,0:T(8,128)} %get-tuple-element.249, s32[1024]{0:T(1024)S(1)} %pad_clamp_fusion.2), kind=kCustom, calls=%fused_computation.clone.clone.1 | custom fusion | bytes 4194816 | tf_op jit(solution)/shard_map/while/body/eval_jaxpr/gather | solution.py:92
  497.5 8.7 %fusion.38 = f32[16,128,768]{2,1,0:T(8,128)} fusion(f32[16,128,64]{2,1,0:T(8,128)S(1)} %get-tuple-element.42, s32[768]{0:T(1024)S(1)} %iota_add_fusion, s32[64]{0:T(128)S(1)} %fusion.61, pred[64]{0:T(512)(128)(4,1)S(1)} %fusion.62), kind=kOutput, calls=%fused_computation.63 | convolution fusion | flops 1208795136 | bytes 6819136 | tf_op jit(solution)/shard_map/dot_general | solution.py:101
  506.2 224.6 %reduce-scatter.2.cloned.1.call-done = f32[1,128,768]{2,1,0:T(8,128)} async-done(((f32[16,128,768]{2,1,0:T(8,128)}), f32[1,128,768]{2,1,0:T(8,128)}) %reduce-scatter.2.cloned.1.call-update) | async-done | bytes 393232 | tf_op jit(solution)/shard_map/reduce_scatter | solution.py:104
  (133 shorter events, 118.6 us)
Async XLA Ops:
  6.5 724.3 %reduce-scatter.2.cloned.1.call-start = ((), (), s32[]{:S(2)}) async-start(), calls=%async_computation.2 | async-start | bytes 6684672 | tf_op jit(solution)/shard_map/reduce_scatter | solution.py:104
  6.7 6.6 copy-start.3
  140.0 53.3 %copy-start = (f32[128,16,4,64]{0,3,2,1:T(8,128)}, f32[128,16,4,64]{0,3,2,1:T(8,128)S(1)}, u32[]{:S(2)}) copy-start(f32[128,16,4,64]{0,3,2,1:T(8,128)S(1)} %copy.50) | copy-start | bytes 6291460
  140.0 44.7 %collective-permute-start = (f32[128,4096]{0,1:T(8,128)S(1)}, f32[128,4096]{0,1:T(8,128)}, u32[]{:S(2)}, u32[]{:S(2)}) collective-permute-start(f32[128,4096]{0,1:T(8,128)S(1)} %bitcast.78), channel_id=1, source_target_pairs={{0,16},{16,32},{32,48},{48,64},{64,80},{80,96},{96,112},{112,128},... | collective-permute-start | bytes 6291464 | tf_op jit(solution)/shard_map/ppermute | solution.py:18
  143.2 48.2 %collective-permute-start.2 = (f32[128,4096]{0,1:T(8,128)S(1)}, f32[128,4096]{0,1:T(8,128)}, u32[]{:S(2)}, u32[]{:S(2)}) collective-permute-start(f32[128,4096]{0,1:T(8,128)S(1)} %bitcast.79), channel_id=1, source_target_pairs={{0,240},{16,0},{32,16},{48,32},{64,48},{80,64},{96,80},{112,96},{1... | collective-permute-start | bytes 6291464 | tf_op jit(solution)/shard_map/ppermute | solution.py:18
  184.8 40.7 %collective-permute-start.1 = (f32[128,4096]{0,1:T(8,128)}, f32[128,4096]{0,1:T(8,128)}, u32[]{:S(2)}, u32[]{:S(2)}) collective-permute-start(f32[128,4096]{0,1:T(8,128)} %collective-permute-done), channel_id=1, source_target_pairs={{0,16},{16,32},{32,48},{48,64},{64,80},{80,96},{96,112},{112,128},... | collective-permute-start | bytes 6291464 | tf_op jit(solution)/shard_map/ppermute | solution.py:18
  191.4 48.2 %collective-permute-start.3 = (f32[128,4096]{0,1:T(8,128)}, f32[128,4096]{0,1:T(8,128)}, u32[]{:S(2)}, u32[]{:S(2)}) collective-permute-start(f32[128,4096]{0,1:T(8,128)} %collective-permute-done.2), channel_id=1, source_target_pairs={{0,240},{16,0},{32,16},{48,32},{64,48},{80,64},{96,80},{112,96},{1... | collective-permute-start | bytes 6291464 | tf_op jit(solution)/shard_map/ppermute | solution.py:18
  228.8 3.4 copy-start.1
  243.0 20.2 %copy-start.2 = (f32[16,128,64]{2,1,0:T(8,128)S(1)}, f32[16,128,64]{2,1,0:T(8,128)}, u32[]{:S(2)}) copy-start(f32[16,128,64]{2,1,0:T(8,128)} %custom-call.4) | copy-start | bytes 1572868
Sparse Core Ops, SparseCore 0:
  506.3 224.4 reduce-scatter.1
where the time goes:
time: 747 us; the launch traced here: 738 us
  waiting for transfers between devices  299 us (40%)
  local copies, waits for them, and re-layouts  242 us (32%)
  other arithmetic  78.7 us (11%)
  blocking collectives  60.5 us (8%)
  matrix products  36.8 us (5%)
  between operations  13.8 us (2%)
    reduce_scatter x1, waiting for transfers between devices, local(): lax.psum_scatter(result.reshape(lax.axis_size('inner') * (PAIRS // groups...  225 us
    gather x16, local copies, waits for them, and re-layouts, one_pair(): partner = extended[local_ids + column_offsets]  156 us
    ppermute x4, waiting for transfers between devices, shifted(): return lax.ppermute(value, axis, pairs)  74.1 us
    reduce_sum x16, other arithmetic, one_pair(): jnp.sum(own_re * partner_re + own_im * partner_im, axis=1) / segment_count  64.9 us
    all_to_all x1, blocking collectives, local(): lax.all_to_all(whitened, 'inner', split_axis=2, concat_axis=1, tiled=True)  60.5 us
    unnamed x18, local copies, waits for them, and re-layouts  44.6 us
    dot_general x1, matrix products, local(): jnp.dot(segment_rows, forward, precision=lax.Precision.HIGHEST, preferred...  26 us
  transfers between devices with their start and end apart: 5, of which 5 were waited for; matrix products, arithmetic and copies ran while one was open for 3% of the time, Pallas kernels for 0%

commit v1 on v0

v1 whole, which is shorter than its diff:
```python
import math

import ml_dtypes
import numpy as np

import jax
import jax.numpy as jnp
from jax import lax
from jax.experimental import pallas as pl
from jax.experimental.pallas import tpu as pltpu
from jax.sharding import PartitionSpec as P

SEG = 1024
SLOT = 2048
LAGS = 768
HALF = 32
PAIRS = 16
F = 512
SEP = 256
CUT = SEG + 128
LANES = 128


def split_table():
    samples = np.arange(SEG // 2, dtype=np.int64)
    rows = []
    for parity in range(2):
        bins = 2 * np.arange(F // 2, dtype=np.int64) + parity
        angle = 2.0 * np.pi / SEG * (bins[:, None] * samples[None, :] % SEG)
        rows += [np.cos(angle), -np.sin(angle)]
    table = np.concatenate(rows, 0).astype(np.float32)
    high = table.astype(ml_dtypes.bfloat16)
    low = (table - high.astype(np.float32)).astype(ml_dtypes.bfloat16)
    return high, low


def split(value):
    high = value.astype(jnp.bfloat16)
    low = (value - high.astype(jnp.float32)).astype(jnp.bfloat16)
    return high, low


def dot3(left, right, dims):
    left_high, left_low = left
    right_high, right_low = right

    def one(a, b):
        return lax.dot_general(a, b, (dims, ((), ())), preferred_element_type=jnp.float32)

    return one(left_high, right_high) + (one(left_high, right_low) + one(left_low, right_high))


def whiten_kernel(starts_ref, window_ref, high_ref, low_ref, records_ref, out_ref, cut_ref, band_ref, sems):
    segments = records_ref.shape[1]
    half = SEG // 2
    quarter = F // 2

    def copy(segment):
        first = lax.min(starts_ref[segment] // LANES, (SLOT - CUT) // LANES) * LANES
        return pltpu.make_async_copy(
            records_ref.at[:, segment, pl.ds(pl.multiple_of(first, LANES), CUT)],
            cut_ref.at[segment],
            sems.at[segment],
        )

    for segment in range(segments):
        copy(segment).start()
    row_ids = lax.broadcasted_iota(jnp.int32, (F, F), 0)
    column_ids = lax.broadcasted_iota(jnp.int32, (F, F), 1)
    row_bins = row_ids % quarter * 2 + row_ids // quarter
    column_bins = column_ids % quarter * 2 + column_ids // quarter
    distance = jnp.abs(row_bins - column_bins)
    distance = jnp.minimum(distance, F - distance)
    band_ref[...] = jnp.where(distance <= HALF, 1.0, 0.0).astype(jnp.bfloat16)
    contract_last = ((1,), (1,))
    for segment in range(segments):
        copy(segment).wait()
        begin = starts_ref[segment]
        first = lax.min(begin // LANES, (SLOT - CUT) // LANES) * LANES
        rolled = pltpu.roll(cut_ref[segment], lax.rem(CUT - (begin - first), CUT), 1)
        piece = rolled[:, :SEG] * window_ref[...]
        folded = (split(piece[:, :half] + piece[:, half:]), split(piece[:, :half] - piece[:, half:]))
        parts = []
        for parity in range(2):
            rows = pl.ds(parity * 2 * quarter, 2 * quarter)
            parts.append(dot3((high_ref[rows, :], low_ref[rows, :]), folded[parity], contract_last))
        power = jnp.concatenate(
            [part[:quarter] * part[:quarter] + part[quarter:] * part[quarter:] for part in parts], 0
        )
        power_high, power_low = split(power)
        band = band_ref[...]
        smooth = jnp.dot(band, power_high, preferred_element_type=jnp.float32) + jnp.dot(
            band, power_low, preferred_element_type=jnp.float32
        )
        scale = lax.rsqrt(smooth * (1.0 / (2 * HALF + 1)) + 1e-06)
        for parity in range(2):
            part_scale = scale[parity * quarter : (parity + 1) * quarter]
            for component in range(2):
                row = (parity * 2 + component) * segments + segment
                value = parts[parity][component * quarter : (component + 1) * quarter] * part_scale
                out_ref[pl.ds(row, quarter, stride=4 * segments), :] = value


def pair_kernel(offsets_ref, white_ref, out_ref, high_ref, low_ref, left_high_ref, left_low_ref, gram_ref):
    blocks, rows, channels = white_ref.shape
    segments = 4
    row_ids = lax.broadcasted_iota(jnp.int32, (rows, channels), 0)
    component = row_ids // segments % 4
    is_imag = component % 2 == 1
    parity = component // 2
    reach = SEP // channels
    width = (2 * reach + 1) * channels

    def fill(block, _):
        value = white_ref[block]
        high, low = split(value)
        high_ref[block] = high
        low_ref[block] = low
        up = pltpu.roll(value, rows - segments, 0)
        down = pltpu.roll(value, segments, 0)
        swapped = jnp.where(is_imag, -down, up)
        high_swapped, low_swapped = split(swapped)
        zero = jnp.zeros_like(high)
        for which in range(2):
            keep = parity == which
            left_high_ref[block, :, pl.ds(which * 2 * channels, channels)] = jnp.where(keep, high, zero)
            left_low_ref[block, :, pl.ds(which * 2 * channels, channels)] = jnp.where(keep, low, zero)
            left_high_ref[block, :, pl.ds((which * 2 + 1) * channels, channels)] = jnp.where(
                keep, high_swapped, zero
            )
            left_low_ref[block, :, pl.ds((which * 2 + 1) * channels, channels)] = jnp.where(
                keep, low_swapped, zero
            )
        return 0

    lax.fori_loop(0, blocks, fill, 0)
    lane_ids = lax.broadcasted_iota(jnp.int32, (channels, channels), 1)
    group = lane_ids // PAIRS
    contract_first = ((0,), (0,))

    def one_block(block, _):
        left = (left_high_ref[block], left_low_ref[block])
        index = offsets_ref[block]
        where_block = index // channels
        lane = index % channels
        picked = jnp.zeros((channels, channels), jnp.float32)
        for step in range(2 * reach + 1):
            other = lax.rem(block + blocks + step - reach, blocks)
            gram = dot3(left, (high_ref[other], low_ref[other]), contract_first)
            hit = where_block == step
            for which in range(4):
                found = jnp.take_along_axis(
                    gram[which * channels : (which + 1) * channels], lane, axis=1, mode="promise_in_bounds"
                )
                picked = jnp.where(hit & (group == which), found, picked)
        out_ref[block] = picked.T[: 4 * PAIRS]
        return 0

    lax.fori_loop(0, blocks, one_block, 0)


def lag_kernel(high_ref, low_ref, cross_ref, out_ref):
    half = SEG // 2
    quarter = F // 2
    sums = []
    for parity in range(2):
        total = None
        for component in range(2):
            place = parity * 2 + component
            value = split(cross_ref[pl.ds(place, quarter, stride=4), :])
            rows = pl.ds(place * quarter, quarter)
            term = dot3(value, (high_ref[rows, :], low_ref[rows, :]), ((0,), (0,)))
            total = term if total is None else total + term
        sums.append(total)
    even, odd = sums
    shift = LAGS // 2
    out_ref[0, :, pl.ds(0, shift)] = (even - odd)[:, half - shift :]
    out_ref[0, :, pl.ds(shift, shift)] = (even + odd)[:, :shift]


def local(records, starts, offsets):
    channels, segments, _ = records.shape
    blocks = lax.axis_size("blk")
    inner = lax.axis_size("inner")
    devices = blocks * inner
    rows = 4 * segments
    high, low = split_table()
    high, low = jnp.asarray(high), jnp.asarray(low)
    samples = np.arange(SEG)
    window = jnp.asarray((0.5 - 0.5 * np.cos(2.0 * np.pi * samples / SEG)).astype(np.float32)[None, :])
    vmem = pl.BlockSpec(memory_space=pltpu.VMEM)
    smem = pl.BlockSpec(memory_space=pltpu.SMEM)
    white = pl.pallas_call(
        whiten_kernel,
        out_shape=jax.ShapeDtypeStruct((devices * rows, channels), jnp.float32),
        in_specs=[smem, vmem, vmem, vmem, pl.BlockSpec(memory_space=pl.ANY)],
        out_specs=vmem,
        scratch_shapes=[
            pltpu.VMEM((segments, channels, CUT), jnp.float32),
            pltpu.VMEM((F, F), jnp.bfloat16),
            pltpu.SemaphoreType.DMA((segments,)),
        ],
        compiler_params=pltpu.CompilerParams(vmem_limit_bytes=40 << 20),
    )(starts, window, high, low, records)
    axes = ("blk", "inner")
    white = lax.all_to_all(white.reshape(devices, rows, channels), axes, split_axis=0, concat_axis=0, tiled=True)
    place = offsets + (jnp.arange(channels, dtype=jnp.int32) + SEP)[:, None]
    place = lax.all_gather(place, "blk", axis=0, tiled=True).reshape(blocks, channels, PAIRS)
    place = jnp.tile(place, (1, 1, channels // PAIRS))
    cross = pl.pallas_call(
        pair_kernel,
        out_shape=jax.ShapeDtypeStruct((blocks, 4 * PAIRS, channels), jnp.float32),
        in_specs=[vmem, vmem],
        out_specs=vmem,
        scratch_shapes=[
            pltpu.VMEM((blocks, inner * rows, channels), jnp.bfloat16),
            pltpu.VMEM((blocks, inner * rows, channels), jnp.bfloat16),
            pltpu.VMEM((blocks, inner * rows, 4 * channels), jnp.bfloat16),
            pltpu.VMEM((blocks, inner * rows, 4 * channels), jnp.bfloat16),
            pltpu.VMEM((8, 128), jnp.float32),
        ],
        compiler_params=pltpu.CompilerParams(vmem_limit_bytes=40 << 20),
    )(place, white.reshape(blocks, inner * rows, channels))
    cross = cross.reshape(blocks, 4, PAIRS, channels).transpose(0, 2, 1, 3).reshape(devices, 4, channels)
    segment_count = inner * segments
    cross = cross * (math.sqrt(segment_count / F) / segment_count)
    cross = lax.all_to_all(cross, axes, split_axis=0, concat_axis=0, tiled=True)
    return pl.pallas_call(
        lag_kernel,
        out_shape=jax.ShapeDtypeStruct((1, channels, LAGS), jnp.float32),
        in_specs=[vmem, vmem, vmem],
        out_specs=vmem,
        compiler_params=pltpu.CompilerParams(vmem_limit_bytes=40 << 20),
    )(high, low, cross.reshape(devices * 4, channels))


def solution(mesh):
    placed = (P("blk", "inner", None), P("inner"), P("blk", None))
    return jax.shard_map(
        local, mesh=mesh, in_specs=placed, out_specs=P("inner", "blk", None), check_vma=False
    )
```

time: 747 us -> 144 us (0.19); the launches traced: 738 us -> 144 us
  waiting for transfers between devices: 299 us -> 31 us
  local copies, waits for them, and re-layouts: 242 us -> 10.2 us
  other arithmetic: 78.7 us -> 0.06 us
  Pallas kernels: 0 us -> 38.8 us
  matrix products: 36.8 us -> 0 us
  between operations: 13.8 us -> 0.1 us
  blocking collectives: 60.5 us -> 48.3 us
  starting transfers between devices: 6.51 us -> 15.7 us
    reduce_scatter x1 -> x0, waiting for transfers between devices: 225 us -> none  [local(): lax.psum_scatter(result.reshape(lax.axis_size('inner') * (PAIRS // groups...]
    gather x28 -> x0, local copies, waits for them, and re-layouts: 169 us -> none  [the longest x16 156 us: one_pair(): partner = extended[local_ids + column_offsets]]
    ppermute x4 -> x0, waiting for transfers between devices: 74.1 us -> none  [shifted(): return lax.ppermute(value, axis, pairs)]
    reduce_sum x16 -> x0, other arithmetic: 64.9 us -> none  [one_pair(): jnp.sum(own_re * partner_re + own_im * partner_im, axis=1) / segment_count]
    pallas_call x0 -> x3, Pallas kernels: none -> 38.8 us  [the longest x1 26.7 us: local(): pl.pallas_call(pair_kernel, out_shape=jax.ShapeDtypeStruct((blocks, 4 * P...]
    unnamed x18, local copies, waits for them, and re-layouts: 44.6 us -> 7.33 us
    dot_general x3 -> x0, matrix products: 36.8 us -> none  [the longest x1 26 us: local(): jnp.dot(segment_rows, forward, precision=lax.Precision.HIGHEST, preferred...]
    all_to_all x1, blocking collectives: 60.5 us -> 27.5 us  [local(): cross = lax.all_to_all(cross, axes, split_axis=0, concat_axis=0, tiled=True)]
  transfers between devices with their start and end apart: 5 -> 1, of which waited for: 5 -> 1; matrix products, arithmetic and copies ran while one was open for 3% -> 2% of each run, Pallas kernels for 0% -> 0%
where the time goes in v1:
time: 144 us
  blocking collectives  48.3 us (34%)
  Pallas kernels  38.8 us (27%)
  waiting for transfers between devices  31 us (22%)
  starting transfers between devices  15.7 us (11%)
  local copies, waits for them, and re-layouts  10.2 us (7%)
    all_to_all x1, waiting for transfers between devices, local(): lax.all_to_all(white.reshape(devices, rows, channels), axes, split_axis=0...  31 us
    all_to_all x1, blocking collectives, local(): cross = lax.all_to_all(cross, axes, split_axis=0, concat_axis=0, tiled=True)  27.5 us
    pallas_call x1, Pallas kernels, local(): pl.pallas_call(pair_kernel, out_shape=jax.ShapeDtypeStruct((blocks, 4 * P...  26.7 us
    all_gather x1, blocking collectives, local(): lax.all_gather(place, 'blk', axis=0, tiled=True)  20.9 us
    all_to_all x1, starting transfers between devices, local(): lax.all_to_all(white.reshape(devices, rows, channels), axes, split_axis=0...  15.7 us
    pallas_call x1, Pallas kernels, local(): pl.pallas_call(whiten_kernel, out_shape=jax.ShapeDtypeStruct((devices * r...  10.7 us
    unnamed x18, local copies, waits for them, and re-layouts  7.33 us
  transfers between devices with their start and end apart: 1, of which 1 were waited for; matrix products, arithmetic and copies ran while one was open for 2% of the time, Pallas kernels for 0%

profile of v1, /device:TPU:1, one launch (start us, length us, event | category | flops | bytes accessed | tf_op | source)
XLA Modules:
  0.0 144.0 jit_solution(3200017514118745530)
XLA Ops:
  0.0 0.0 copy-start.1
  0.0 2.2 %copy-done.1 = f32[128,4,2048]{2,1,0:T(4,128)S(1)} copy-done((f32[128,4,2048]{2,1,0:T(4,128)S(1)}, f32[128,4,2048]{2,1,0:T(4,128)}, u32[]{:S(2)}) %copy-start.1) | copy-done | bytes 4194328
  2.2 0.0 copy-start.2
  2.2 1.2 copy-done.2
  3.4 0.0 copy-start.4
  3.4 1.2 copy-done.4
  4.6 0.0 copy-start.6
  4.6 0.7 copy-done.6
  5.3 0.0 copy-start.7
  5.3 0.7 copy-done.7
  6.0 10.7 %shard_map.64 = f32[4096,128]{1,0:T(8,128)S(1)} custom-call(s32[4]{0:T(128)S(1)} %copy-done.7, f32[1,1024]{1,0:T(1,128)S(1)} %copy-done.6, bf16[1024,512]{1,0:T(8,128)(2,1)S(1)} %copy-done.4, bf16[1024,512]{1,0:T(8,128)(2,1)S(1)} %copy-done.2, f32[128,4,2048]{2,1,0:T(4,128)S(1)} %copy-done.1), custom_call_target="tpu_custom_call" | custom-call | tf_op jit(solution)/shard_map/pallas_call | solution.py:193
  16.7 0.0 copy-start
  16.7 1.3 copy-done
  18.0 0.0 copy-start.8
  18.0 15.7 %all-to-all-start = ((f32[256,16,128]{2,1,0:T(8,128)}), f32[256,16,128]{2,1,0:T(8,128)S(1)}, u32[]{:S(2)}, u32[]{:S(2)}) async-start(f32[256,16,128]{2,1,0:T(8,128)} %bitcast.14), calls=%async_computation | async-start | bytes 4194304 | tf_op jit(solution)/shard_map/all_to_all | solution.py:206
  33.7 0.0 copy-done.8
  33.7 20.9 %all_gather.3 = s32[2048,16]{0,1:T(8,128)S(1)} all-gather(s32[128,16]{0,1:T(8,128)S(1)} %broadcast_add_fusion), channel_id=1, replica_groups=mesh['blk'=16,'inner'=16] {'blk'}, dimensions={0}, use_global_device_ids=true | all-gather | bytes 139264 | tf_op jit(solution)/shard_map/all_gather | solution.py:208
  54.6 1.1 tile.11
  55.7 1.6 %copy.10.offsets_ref = s32[16,128,128]{2,1,0:T(8,128)S(1)} copy(s32[16,128,128]{1,2,0:T(8,128)} %bitcast.16) | data formatting | bytes 2097152 | tf_op jit(solution)/shard_map/tile | solution.py:209
  57.2 31.0 %all-to-all-done = f32[256,16,128]{2,1,0:T(8,128)S(1)} async-done(((f32[256,16,128]{2,1,0:T(8,128)}), f32[256,16,128]{2,1,0:T(8,128)S(1)}, u32[]{:S(2)}, u32[]{:S(2)}) %all-to-all-start) | async-done | bytes 2097184 | tf_op jit(solution)/shard_map/all_to_all | solution.py:206
  88.2 26.7 %shard_map.65 = f32[16,64,128]{2,1,0:T(8,128)S(1)} custom-call(s32[16,128,128]{2,1,0:T(8,128)S(1)} %copy.10.offsets_ref, f32[16,256,128]{2,1,0:T(8,128)S(1)} %bitcast.13), custom_call_target="tpu_custom_call" | custom-call | tf_op jit(solution)/shard_map/pallas_call | solution.py:210
  114.9 0.0 copy-start.3
  114.9 0.0 copy-start.5
  115.0 0.2 copy.11
  115.2 27.5 %all_to_all.10 = f32[256,4,128]{2,1,0:T(4,128)S(1)} all-to-all(f32[256,4,128]{2,1,0:T(4,128)S(1)} %bitcast.18), channel_id=1, replica_groups=mesh['blk'=16,'inner'=16] {'blk','inner'}, dimensions={0} | all-to-all | bytes 1048576 | tf_op jit(solution)/shard_map/all_to_all | solution.py:227
  142.7 0.0 copy-done.3
  142.7 0.0 copy-done.5
  142.7 1.4 shard_map.66
  (4 shorter events, 0.1 us)
Async XLA Ops:
  0.0 2.2 %copy-start.1 = (f32[128,4,2048]{2,1,0:T(4,128)S(1)}, f32[128,4,2048]{2,1,0:T(4,128)}, u32[]{:S(2)}) copy-start(f32[128,4,2048]{2,1,0:T(4,128)} %records_ref.1) | copy-start | bytes 12582916
  2.2 1.2 copy-start.2
  3.4 1.2 copy-start.4
  4.6 0.7 copy-start.6
  5.3 0.7 copy-start.7
  16.7 1.3 copy-start
  18.0 15.7 %copy-start.8 = (s32[128,16]{0,1:T(8,128)S(1)}, s32[128,16]{0,1:T(8,128)}, u32[]{:S(2)}) copy-start(s32[128,16]{0,1:T(8,128)} %param.8) | copy-start | bytes 24580
  18.0 70.2 %all-to-all-start = ((f32[256,16,128]{2,1,0:T(8,128)}), f32[256,16,128]{2,1,0:T(8,128)S(1)}, u32[]{:S(2)}, u32[]{:S(2)}) async-start(f32[256,16,128]{2,1,0:T(8,128)} %bitcast.14), calls=%async_computation | async-start | bytes 4194304 | tf_op jit(solution)/shard_map/all_to_all | solution.py:206
  114.9 27.8 %copy-start.3 = (bf16[1024,512]{1,0:T(8,128)(2,1)S(1)}, bf16[1024,512]{1,0:T(8,128)(2,1)}, u32[]{:S(2)}) copy-start(bf16[1024,512]{1,0:T(8,128)(2,1)} %constant.11.clone.low_ref) | copy-start | bytes 3145732
  114.9 27.8 %copy-start.5 = (bf16[1024,512]{1,0:T(8,128)(2,1)S(1)}, bf16[1024,512]{1,0:T(8,128)(2,1)}, u32[]{:S(2)}) copy-start(bf16[1024,512]{1,0:T(8,128)(2,1)} %constant.10.clone.high_ref) | copy-start | bytes 3145732

commit v2 on v1

v2 whole, which is shorter than its diff:
```python
import math

import ml_dtypes
import numpy as np

import jax
import jax.numpy as jnp
from jax import lax
from jax.experimental import pallas as pl
from jax.experimental.pallas import tpu as pltpu
from jax.sharding import PartitionSpec as P

SEG = 1024
SLOT = 2048
LAGS = 768
HALF = 32
PAIRS = 16
F = 512
SEP = 256
LANES = 128
CUT = SEG + LANES
BLOCKS = 16
INNER = 16
DEVICES = BLOCKS * INNER
SEGMENTS = 4
ROWS = 4 * SEGMENTS
QUARTER = F // 2
REACH = SEP // LANES
SPAN = 2 * REACH + 1
AHEAD = 6
MESH = pl.DeviceIdType.MESH


def split_table():
    samples = np.arange(SEG // 2, dtype=np.int64)
    rows = []
    for parity in range(2):
        bins = 2 * np.arange(QUARTER, dtype=np.int64) + parity
        angle = 2.0 * np.pi / SEG * (bins[:, None] * samples[None, :] % SEG)
        rows += [np.cos(angle), -np.sin(angle)]
    table = np.concatenate(rows, 0).astype(np.float32)
    high = table.astype(ml_dtypes.bfloat16)
    low = (table - high.astype(np.float32)).astype(ml_dtypes.bfloat16)
    return high, low


def split(value):
    high = value.astype(jnp.bfloat16)
    low = (value - high.astype(jnp.float32)).astype(jnp.bfloat16)
    return high, low


def dot(left, right, dims):
    return lax.dot_general(left, right, (dims, ((), ())), preferred_element_type=jnp.float32)


def cut_kernel(starts_hbm, records_ref, out_ref, starts_ref, cut_ref, starts_sem, sems):
    load = pltpu.make_async_copy(starts_hbm, starts_ref, starts_sem)
    load.start()
    load.wait()

    def first_of(segment):
        return lax.min(starts_ref[segment] // LANES, (SLOT - CUT) // LANES) * LANES

    def copy(segment):
        return pltpu.make_async_copy(
            records_ref.at[:, segment, pl.ds(pl.multiple_of(first_of(segment), LANES), CUT)],
            cut_ref.at[segment],
            sems.at[segment],
        )

    for segment in range(SEGMENTS):
        copy(segment).start()
    samples = lax.broadcasted_iota(jnp.int32, (8, SEG), 1).astype(jnp.float32)
    window = (0.5 - 0.5 * jnp.cos(2.0 * jnp.pi / SEG * samples))[:1]
    for segment in range(SEGMENTS):
        copy(segment).wait()
        shift = starts_ref[segment] - first_of(segment)
        rolled = pltpu.roll(cut_ref[segment], lax.rem(CUT - shift, CUT), 1)
        out_ref[segment] = rolled[:, :SEG] * window


def kernel(
    offsets_hbm,
    slots_ref,
    high_ref,
    low_ref,
    out_ref,
    offsets_ref,
    table_ref,
    band_ref,
    send_ref,
    recv_ref,
    place_ref,
    places_ref,
    right_ref,
    found_ref,
    cross_ref,
    offsets_sem,
    table_sems,
    local_sems,
    send_sems,
    recv_sems,
    place_sems,
    cross_sem,
):
    my_block = lax.axis_index("blk")
    my_inner = lax.axis_index("inner")
    me = my_block * INNER + my_inner
    half = SEG // 2

    def load_table(part):
        source = (high_ref, high_ref, low_ref)[part]
        return pltpu.make_async_copy(source, table_ref.at[:, pl.ds(part * half, half)], table_sems.at[part])

    load_offsets = pltpu.make_async_copy(offsets_hbm, offsets_ref, offsets_sem)
    load_offsets.start()
    for part in range(3):
        load_table(part).start()

    barrier = pltpu.get_barrier_semaphore()

    def greet(step, _):
        device = lax.rem(me + step, DEVICES)
        pl.semaphore_signal(
            barrier, inc=1, device_id=(device // INNER, lax.rem(device, INNER)), device_id_type=MESH
        )
        return 0

    lax.fori_loop(1, DEVICES, greet, 0, unroll=5)

    load_offsets.wait()
    channel_ids = lax.broadcasted_iota(jnp.int32, (1, LANES), 1)
    for pair in range(PAIRS):
        row = offsets_ref[pl.ds(pair, 1), :] + (channel_ids + SEP)
        place_ref[pl.ds(4 * pair, 4), :] = jnp.broadcast_to(row, (4, LANES))

    row_ids = lax.broadcasted_iota(jnp.int32, (F, F), 0)
    column_ids = lax.broadcasted_iota(jnp.int32, (F, F), 1)
    row_bins = row_ids % QUARTER * 2 + row_ids // QUARTER
    column_bins = column_ids % QUARTER * 2 + column_ids // QUARTER
    distance = jnp.abs(row_bins - column_bins)
    distance = jnp.minimum(distance, F - distance)
    band = jnp.where(distance <= HALF, 1.0, 0.0).astype(jnp.bfloat16)
    band_ref[:, pl.ds(0, F)] = band
    band_ref[:, pl.ds(F, F)] = band
    for part in range(3):
        load_table(part).wait()

    for first_segment in range(0, SEGMENTS, 2):
        pieces = []
        for segment in range(first_segment, first_segment + 2):
            pieces.append(slots_ref[segment])
        piece = jnp.concatenate(pieces, 0)
        parts = []
        for parity in range(2):
            front, back = piece[:, :half], piece[:, half:]
            high, low = split(front + back if parity == 0 else front - back)
            stacked = jnp.concatenate([high, low, high], 1)
            rows = table_ref[pl.ds(parity * 2 * QUARTER, 2 * QUARTER), :]
            parts.append(dot(rows, stacked, ((1,), (1,))))
        power = jnp.concatenate(
            [part[:QUARTER] * part[:QUARTER] + part[QUARTER:] * part[QUARTER:] for part in parts], 0
        )
        smooth = dot(band_ref[...], jnp.concatenate(split(power), 0), ((1,), (0,)))
        scale = lax.rsqrt(smooth * (1.0 / (2 * HALF + 1)) + 1e-06)
        for parity in range(2):
            part_scale = scale[parity * QUARTER : (parity + 1) * QUARTER]
            for component in range(2):
                value = parts[parity][component * QUARTER : (component + 1) * QUARTER] * part_scale
                for second in range(2):
                    row = (parity * 2 + component) * SEGMENTS + first_segment + second
                    send_ref[pl.ds(row, QUARTER, stride=ROWS), :] = value[:, second * LANES : (second + 1) * LANES]

    pl.semaphore_wait(barrier, DEVICES - 1)

    def chunk(device):
        return pl.ds(pl.multiple_of(device * ROWS, ROWS), ROWS)

    own_chunk = pltpu.make_async_copy(send_ref.at[chunk(me)], recv_ref.at[chunk(me)], local_sems.at[0])
    own_chunk.start()
    own_place = pltpu.make_async_copy(place_ref, places_ref.at[my_block], local_sems.at[1])
    own_place.start()

    def send_step(step):
        block = lax.rem(my_block + step, BLOCKS)

        def send_one(shift, _):
            other = lax.rem(my_inner + shift, INNER)
            pltpu.make_async_remote_copy(
                src_ref=send_ref.at[chunk(block * INNER + other)],
                dst_ref=recv_ref.at[chunk(me)],
                send_sem=send_sems.at[0],
                recv_sem=recv_sems.at[step],
                device_id=(block, other),
                device_id_type=MESH,
            ).start()
            return 0

        lax.fori_loop(1, INNER, send_one, 0)

        @pl.when(step > 0)
        def _():
            send_one(0, 0)
            pltpu.make_async_remote_copy(
                src_ref=place_ref,
                dst_ref=places_ref.at[my_block],
                send_sem=send_sems.at[1],
                recv_sem=place_sems.at[step],
                device_id=(block, my_inner),
                device_id_type=MESH,
            ).start()

    next_device = (lax.rem(my_block + 1, BLOCKS), my_inner)

    def awaited(source, target, send_sem, recv_sem):
        return pltpu.make_async_remote_copy(
            src_ref=source,
            dst_ref=target,
            send_sem=send_sem,
            recv_sem=recv_sem,
            device_id=next_device,
            device_id_type=MESH,
        )

    block_rows = INNER * ROWS
    lanes = lax.broadcasted_iota(jnp.int32, (LANES, LANES), 1)
    flips = lax.broadcasted_iota(jnp.int32, (INNER, 2 * SEGMENTS, LANES), 1) < SEGMENTS

    def block_of(step):
        return lax.rem(my_block + BLOCKS - step, BLOCKS)

    def block_values(block):
        values = recv_ref[pl.ds(pl.multiple_of(block * block_rows, block_rows), block_rows), :]
        return values.reshape(INNER, ROWS, LANES)

    def receive(step):
        @pl.when(step == 0)
        def _():
            own_chunk.wait()
            own_place.wait()
            awaited(
                send_ref.at[pl.ds(0, block_rows - ROWS)],
                recv_ref.at[pl.ds(0, block_rows - ROWS)],
                send_sems.at[0],
                recv_sems.at[0],
            ).wait_recv()

        @pl.when(step > 0)
        def _():
            awaited(
                send_ref.at[pl.ds(0, block_rows)],
                recv_ref.at[pl.ds(0, block_rows)],
                send_sems.at[0],
                recv_sems.at[step],
            ).wait_recv()
            awaited(place_ref, places_ref.at[0], send_sems.at[1], place_sems.at[step]).wait_recv()

        values = block_values(block_of(step))
        for parity in range(2):
            value = values[:, parity * 2 * SEGMENTS : (parity + 1) * 2 * SEGMENTS, :].reshape(LANES, LANES)
            high, low = split(value)
            stacked = jnp.concatenate([high, low, high], 0)

            def place_at(slot):
                right_ref[parity, :, pl.ds(pl.multiple_of(slot * LANES, LANES), LANES)] = stacked

            place_at(BLOCKS + 1 - step)

            @pl.when(step < 2)
            def _():
                place_at(1 - step)

            @pl.when(step >= BLOCKS - 2)
            def _():
                place_at(BLOCKS + 1 - step + BLOCKS)

    def correlate(step):
        block = block_of(step)
        values = block_values(block)
        place = jnp.concatenate([places_ref[block], jnp.zeros((LANES - 4 * PAIRS, LANES), jnp.int32)], 0).T
        lane = place % LANES
        code = place // LANES * 4 + lanes % 4
        picked = jnp.zeros((LANES, LANES), jnp.float32)
        columns = pl.ds(pl.multiple_of((BLOCKS - 1 - step) * LANES, LANES), SPAN * LANES)
        for parity in range(2):
            value = values[:, parity * 2 * SEGMENTS : (parity + 1) * 2 * SEGMENTS, :]
            turned = pltpu.roll(value, SEGMENTS, 1)
            turned = jnp.where(flips, turned, -turned)
            left = jnp.concatenate([value.reshape(LANES, LANES).T, turned.reshape(LANES, LANES).T], 0)
            high, low = split(left)
            gram = dot(jnp.concatenate([high, high, low], 1), right_ref[parity, :, columns], ((1,), (0,)))
            for component in range(2):
                for near in range(SPAN):
                    tile = gram[
                        component * LANES : (component + 1) * LANES, near * LANES : (near + 1) * LANES
                    ]
                    value_there = jnp.take_along_axis(tile, lane, axis=1, mode="promise_in_bounds")
                    picked = jnp.where(code == near * 4 + parity * 2 + component, value_there, picked)
        picked = picked.T
        for pair in range(PAIRS):
            found_ref[step, pair] = picked[4 * pair : 4 * pair + 4]

        def send_pair(shift, _):
            pair = lax.rem(my_inner + shift, INNER)
            pltpu.make_async_remote_copy(
                src_ref=found_ref.at[step, pair],
                dst_ref=cross_ref.at[me],
                send_sem=send_sems.at[2],
                recv_sem=cross_sem,
                device_id=(block, pair),
                device_id_type=MESH,
            ).start()
            return 0

        lax.fori_loop(1, INNER, send_pair, 0)

        @pl.when(step > 0)
        def _():
            send_pair(0, 0)

    def first_sends(step, _):
        send_step(step)
        return 0

    lax.fori_loop(0, AHEAD, first_sends, 0)

    def round_trip(turn, _):
        @pl.when(turn < BLOCKS - AHEAD)
        def _():
            send_step(turn + AHEAD)

        @pl.when(turn < BLOCKS)
        def _():
            receive(turn)

        @pl.when(turn >= 2 * REACH)
        def _():
            correlate(lax.rem(turn - REACH, BLOCKS))

        return 0

    lax.fori_loop(0, BLOCKS + 2 * REACH, round_trip, 0)

    own_cross = pltpu.make_async_copy(found_ref.at[0, my_inner], cross_ref.at[me], local_sems.at[2])
    own_cross.start()
    own_cross.wait()
    awaited(
        cross_ref.at[pl.ds(0, DEVICES - 1)], cross_ref.at[pl.ds(0, DEVICES - 1)], send_sems.at[2], cross_sem
    ).wait_recv()

    sums = []
    for parity in range(2):
        total = None
        for component in range(2):
            place = parity * 2 + component
            high, low = split(cross_ref[:, place, :])
            rows = table_ref[pl.ds(place * QUARTER, QUARTER), :]
            table_high, table_low = rows[:, :half], rows[:, 2 * half :]
            first = ((0,), (0,))
            term = dot(high, table_high, first) + (dot(high, table_low, first) + dot(low, table_high, first))
            total = term if total is None else total + term
        sums.append(total)
    even, odd = sums
    shift = LAGS // 2
    segment_count = INNER * SEGMENTS
    factor = math.sqrt(segment_count / F) / segment_count
    out_ref[0, :, pl.ds(0, shift)] = (even - odd)[:, half - shift :] * factor
    out_ref[0, :, pl.ds(shift, shift)] = (even + odd)[:, :shift] * factor

    rest = DEVICES * ROWS - ROWS
    awaited(send_ref.at[pl.ds(0, rest)], recv_ref.at[pl.ds(0, rest)], send_sems.at[0], recv_sems.at[0]).wait_send()
    awaited(
        places_ref.at[pl.ds(0, BLOCKS - 1)], places_ref.at[pl.ds(0, BLOCKS - 1)], send_sems.at[1], place_sems.at[0]
    ).wait_send()
    awaited(
        cross_ref.at[pl.ds(0, DEVICES - 1)], cross_ref.at[pl.ds(0, DEVICES - 1)], send_sems.at[2], cross_sem
    ).wait_send()


def local(records, starts, offsets):
    high, low = split_table()
    vmem = pl.BlockSpec(memory_space=pltpu.VMEM)
    hbm = pl.BlockSpec(memory_space=pltpu.HBM)
    dma = pltpu.SemaphoreType.DMA
    pieces = pl.pallas_call(
        cut_kernel,
        out_shape=jax.ShapeDtypeStruct((SEGMENTS, LANES, SEG), jnp.float32),
        in_specs=[hbm, hbm],
        out_specs=vmem,
        scratch_shapes=[
            pltpu.SMEM((SEGMENTS,), jnp.int32),
            pltpu.VMEM((SEGMENTS, LANES, CUT), jnp.float32),
            dma,
            dma((SEGMENTS,)),
        ],
        compiler_params=pltpu.CompilerParams(vmem_limit_bytes=56 << 20),
    )(starts, records)
    return pl.pallas_call(
        kernel,
        out_shape=jax.ShapeDtypeStruct((1, LANES, LAGS), jnp.float32),
        in_specs=[hbm, vmem, hbm, hbm],
        out_specs=vmem,
        scratch_shapes=[
            pltpu.VMEM((PAIRS, LANES), jnp.int32),
            pltpu.VMEM((2 * F, 3 * (SEG // 2)), jnp.bfloat16),
            pltpu.VMEM((F, 2 * F), jnp.bfloat16),
            pltpu.VMEM((DEVICES * ROWS, LANES), jnp.float32),
            pltpu.VMEM((DEVICES * ROWS, LANES), jnp.float32),
            pltpu.VMEM((4 * PAIRS, LANES), jnp.int32),
            pltpu.VMEM((BLOCKS, 4 * PAIRS, LANES), jnp.int32),
            pltpu.VMEM((2, 3 * LANES, (BLOCKS + 2 * REACH) * LANES), jnp.bfloat16),
            pltpu.VMEM((BLOCKS, PAIRS, 4, LANES), jnp.float32),
            pltpu.VMEM((DEVICES, 4, LANES), jnp.float32),
            dma,
            dma((3,)),
            dma((3,)),
            dma((3,)),
            dma((BLOCKS,)),
            dma((BLOCKS,)),
            dma,
        ],
        compiler_params=pltpu.CompilerParams(
            collective_id=0, has_side_effects=True, vmem_limit_bytes=58 << 20
        ),
    )(offsets.T, pieces, jnp.asarray(high), jnp.asarray(low))


def solution(mesh):
    placed = (P("blk", "inner", None), P("inner"), P("blk", None))
    return jax.shard_map(
        local, mesh=mesh, in_specs=placed, out_specs=P("inner", "blk", None), check_vma=False
    )
```

time: 144 us -> 92.5 us (0.64)
  Pallas kernels: 38.8 us -> 89.5 us
  blocking collectives: 48.3 us -> 0 us
  waiting for transfers between devices: 31 us -> 0 us
  starting transfers between devices: 15.7 us -> 0 us
  local copies, waits for them, and re-layouts: 10.2 us -> 1.77 us
    pallas_call x3 -> x2, Pallas kernels: 38.8 us -> 89.5 us  [the longest x1 85.1 us: local(): pl.pallas_call(kernel, out_shape=jax.ShapeDtypeStruct((1, LANES, LAGS), j...]
    all_to_all x1 -> x0, waiting for transfers between devices: 31 us -> none  [local(): lax.all_to_all(white.reshape(devices, rows, channels), axes, split_axis=0...]
    all_to_all x1 -> x0, blocking collectives: 27.5 us -> none  [local(): cross = lax.all_to_all(cross, axes, split_axis=0, concat_axis=0, tiled=True)]
    all_gather x1 -> x0, blocking collectives: 20.9 us -> none  [local(): lax.all_gather(place, 'blk', axis=0, tiled=True)]
    all_to_all x1 -> x0, starting transfers between devices: 15.7 us -> none  [local(): lax.all_to_all(white.reshape(devices, rows, channels), axes, split_axis=0...]
    unnamed x18 -> x1, local copies, waits for them, and re-layouts: 7.33 us -> 1.77 us
    another operation x3 -> x0, local copies, waits for them, and re-layouts: 2.63 us -> none  [local(): place = jnp.tile(place, (1, 1, channels // PAIRS))]
  transfers between devices with their start and end apart: 1 -> 0, of which waited for: 1 -> 0; matrix products, arithmetic and copies ran while one was open for 2% -> 0% of each run, Pallas kernels for 0% -> 0%
where the time goes in v2:
time: 92.5 us; the launch traced here: 91.3 us
  Pallas kernels  89.5 us (97%)
  local copies, waits for them, and re-layouts  1.77 us (2%)
    pallas_call x1, Pallas kernels, local(): pl.pallas_call(kernel, out_shape=jax.ShapeDtypeStruct((1, LANES, LAGS), j...  85.1 us
    pallas_call x1, Pallas kernels, local(): pl.pallas_call(cut_kernel, out_shape=jax.ShapeDtypeStruct((SEGMENTS, LANE...  4.42 us

profile of v2, /device:TPU:1, one launch (start us, length us, event | category | flops | bytes accessed | tf_op | source)
XLA Modules:
  0.0 91.3 jit_solution(834568159517343318)
XLA Ops:
  0.0 4.4 %shard_map.55.slots_ref = f32[4,128,1024]{2,1,0:T(8,128)} custom-call(s32[4]{0:T(128)} %starts_hbm.1, f32[128,4,2048]{2,1,0:T(4,128)} %records_ref.1), custom_call_target="tpu_custom_call" | custom-call | tf_op jit(solution)/shard_map/pallas_call | solution.py:386
  4.4 85.1 %shard_map.56 = f32[1,128,768]{2,1,0:T(8,128)} custom-call(s32[16,128]{1,0:T(8,128)} %bitcast.1, f32[4,128,1024]{2,1,0:T(8,128)} %shard_map.55.slots_ref, bf16[1024,512]{1,0:T(8,128)(2,1)} %constant.4.clone.high_ref, bf16[1024,512]{1,0:T(8,128)(2,1)} %constant.5.clone.low_ref), custom_call_target="tpu_custom_call" | custom-call | tf_op jit(solution)/shard_map/pallas_call | solution.py:399
  89.5 1.8 %copy.7 = f32[1,128,768]{2,1,0:T(8,128)} copy(f32[1,128,768]{2,1,0:T(8,128)} %shard_map.56) | data formatting | bytes 786432

commit v3 on v2

--- a/solution.py
+++ b/solution.py
@@ -27,7 +27,6 @@
 QUARTER = F // 2
 REACH = SEP // LANES
 SPAN = 2 * REACH + 1
-AHEAD = 6
 MESH = pl.DeviceIdType.MESH
 
 
@@ -54,39 +53,16 @@
     return lax.dot_general(left, right, (dims, ((), ())), preferred_element_type=jnp.float32)
 
 
-def cut_kernel(starts_hbm, records_ref, out_ref, starts_ref, cut_ref, starts_sem, sems):
-    load = pltpu.make_async_copy(starts_hbm, starts_ref, starts_sem)
-    load.start()
-    load.wait()
-
-    def first_of(segment):
-        return lax.min(starts_ref[segment] // LANES, (SLOT - CUT) // LANES) * LANES
-
-    def copy(segment):
-        return pltpu.make_async_copy(
-            records_ref.at[:, segment, pl.ds(pl.multiple_of(first_of(segment), LANES), CUT)],
-            cut_ref.at[segment],
-            sems.at[segment],
-        )
-
-    for segment in range(SEGMENTS):
-        copy(segment).start()
-    samples = lax.broadcasted_iota(jnp.int32, (8, SEG), 1).astype(jnp.float32)
-    window = (0.5 - 0.5 * jnp.cos(2.0 * jnp.pi / SEG * samples))[:1]
-    for segment in range(SEGMENTS):
-        copy(segment).wait()
-        shift = starts_ref[segment] - first_of(segment)
-        rolled = pltpu.roll(cut_ref[segment], lax.rem(CUT - shift, CUT), 1)
-        out_ref[segment] = rolled[:, :SEG] * window
-
-
 def kernel(
+    starts_hbm,
     offsets_hbm,
-    slots_ref,
+    records_ref,
     high_ref,
     low_ref,
     out_ref,
+    starts_ref,
     offsets_ref,
+    slots_ref,
     table_ref,
     band_ref,
     send_ref,
@@ -96,13 +72,15 @@
     right_ref,
     found_ref,
     cross_ref,
-    offsets_sem,
+    index_sems,
+    load_sems,
     table_sems,
     local_sems,
     send_sems,
     recv_sems,
     place_sems,
     cross_sem,
+    row_sem,
 ):
     my_block = lax.axis_index("blk")
     my_inner = lax.axis_index("inner")
@@ -113,21 +91,34 @@
         source = (high_ref, high_ref, low_ref)[part]
         return pltpu.make_async_copy(source, table_ref.at[:, pl.ds(part * half, half)], table_sems.at[part])
 
-    load_offsets = pltpu.make_async_copy(offsets_hbm, offsets_ref, offsets_sem)
+    def load_segment(segment):
+        return pltpu.make_async_copy(records_ref.at[:, segment, :], slots_ref.at[segment], load_sems.at[segment])
+
+    load_starts = pltpu.make_async_copy(starts_hbm, starts_ref, index_sems.at[0])
+    load_offsets = pltpu.make_async_copy(offsets_hbm, offsets_ref, index_sems.at[1])
+    load_starts.start()
     load_offsets.start()
+    for segment in range(2):
+        load_segment(segment).start()
     for part in range(3):
         load_table(part).start()
+    for segment in range(2, SEGMENTS):
+        load_segment(segment).start()
 
     barrier = pltpu.get_barrier_semaphore()
 
+    def peer_in_row(step):
+        return (my_block, (my_inner + step) & (INNER - 1))
+
+    def peer_in_column(step):
+        return ((my_block + step) & (BLOCKS - 1), my_inner)
+
     def greet(step, _):
-        device = lax.rem(me + step, DEVICES)
-        pl.semaphore_signal(
-            barrier, inc=1, device_id=(device // INNER, lax.rem(device, INNER)), device_id_type=MESH
-        )
+        pl.semaphore_signal(barrier, inc=1, device_id=peer_in_row(step), device_id_type=MESH)
+        pl.semaphore_signal(barrier, inc=1, device_id=peer_in_column(step), device_id_type=MESH)
         return 0
 
-    lax.fori_loop(1, DEVICES, greet, 0, unroll=5)
+    lax.fori_loop(1, INNER, greet, 0)
 
     load_offsets.wait()
     channel_ids = lax.broadcasted_iota(jnp.int32, (1, LANES), 1)
@@ -135,22 +126,44 @@
         row = offsets_ref[pl.ds(pair, 1), :] + (channel_ids + SEP)
         place_ref[pl.ds(4 * pair, 4), :] = jnp.broadcast_to(row, (4, LANES))
 
-    row_ids = lax.broadcasted_iota(jnp.int32, (F, F), 0)
-    column_ids = lax.broadcasted_iota(jnp.int32, (F, F), 1)
-    row_bins = row_ids % QUARTER * 2 + row_ids // QUARTER
-    column_bins = column_ids % QUARTER * 2 + column_ids // QUARTER
-    distance = jnp.abs(row_bins - column_bins)
-    distance = jnp.minimum(distance, F - distance)
-    band = jnp.where(distance <= HALF, 1.0, 0.0).astype(jnp.bfloat16)
-    band_ref[:, pl.ds(0, F)] = band
-    band_ref[:, pl.ds(F, F)] = band
+    gap = 2 * (
+        lax.broadcasted_iota(jnp.int32, (QUARTER, QUARTER), 0) - lax.broadcasted_iota(jnp.int32, (QUARTER, QUARTER), 1)
+    )
+
+    def near_bins(shift):
+        distance = jnp.abs(gap + shift)
+        distance = jnp.minimum(distance, F - distance)
+        return jnp.where(distance <= HALF, 1.0, 0.0).astype(jnp.bfloat16)
+
+    same, after, before = near_bins(0), near_bins(1), near_bins(-1)
+    for copy in range(2):
+        band_ref[pl.ds(0, QUARTER), pl.ds(copy * F, QUARTER)] = same
+        band_ref[pl.ds(0, QUARTER), pl.ds(copy * F + QUARTER, QUARTER)] = before
+        band_ref[pl.ds(QUARTER, QUARTER), pl.ds(copy * F, QUARTER)] = after
+        band_ref[pl.ds(QUARTER, QUARTER), pl.ds(copy * F + QUARTER, QUARTER)] = same
+    samples = lax.broadcasted_iota(jnp.int32, (8, SEG), 1).astype(jnp.float32)
+    window = (0.5 - 0.5 * jnp.cos(2.0 * jnp.pi / SEG * samples))[:1]
+    load_starts.wait()
+    lanes = lax.broadcasted_iota(jnp.int32, (LANES, LANES), 1)
     for part in range(3):
         load_table(part).wait()
 
-    for first_segment in range(0, SEGMENTS, 2):
+    def transform(first_segment):
         pieces = []
         for segment in range(first_segment, first_segment + 2):
-            pieces.append(slots_ref[segment])
+            load_segment(segment).wait()
+            begin = jnp.full((LANES, LANES), starts_ref[segment], jnp.int32)
+            first = jnp.minimum(begin >> 7, (SLOT - CUT) // LANES)
+            tiles = [slots_ref[segment, :, pl.ds(at, LANES)] for at in range(0, SLOT, LANES)]
+            for bit, kept in ((4, CUT // LANES + 3), (2, CUT // LANES + 1), (1, CUT // LANES)):
+                moved = (first & bit) != 0
+                tiles = [jnp.where(moved, tiles[at + bit], tiles[at]) for at in range(kept)]
+            place = lanes + (begin - first * LANES)
+            stays = place < LANES
+            place = place & (LANES - 1)
+            turned = [jnp.take_along_axis(tile, place, axis=1, mode="promise_in_bounds") for tile in tiles]
+            piece = [jnp.where(stays, turned[at], turned[at + 1]) for at in range(SEG // LANES)]
+            pieces.append(jnp.concatenate(piece, 1) * window)
         piece = jnp.concatenate(pieces, 0)
         parts = []
         for parity in range(2):
@@ -172,7 +185,16 @@
                     row = (parity * 2 + component) * SEGMENTS + first_segment + second
                     send_ref[pl.ds(row, QUARTER, stride=ROWS), :] = value[:, second * LANES : (second + 1) * LANES]
 
-    pl.semaphore_wait(barrier, DEVICES - 1)
+    transform(0)
+    pl.semaphore_wait(barrier, 2 * (INNER - 1))
+
+    def pass_on(step, _):
+        pl.semaphore_signal(row_sem, inc=1, device_id=peer_in_column(step), device_id_type=MESH)
+        return 0
+
+    lax.fori_loop(1, BLOCKS, pass_on, 0)
+    transform(2)
+    pl.semaphore_wait(row_sem, BLOCKS - 1)
 
     def chunk(device):
         return pl.ds(pl.multiple_of(device * ROWS, ROWS), ROWS)
@@ -224,7 +246,6 @@
         )
 
     block_rows = INNER * ROWS
-    lanes = lax.broadcasted_iota(jnp.int32, (LANES, LANES), 1)
     flips = lax.broadcasted_iota(jnp.int32, (INNER, 2 * SEGMENTS, LANES), 1) < SEGMENTS
 
     def block_of(step):
@@ -319,17 +340,13 @@
         def _():
             send_pair(0, 0)
 
-    def first_sends(step, _):
+    def all_sends(step, _):
         send_step(step)
         return 0
 
-    lax.fori_loop(0, AHEAD, first_sends, 0)
+    lax.fori_loop(0, BLOCKS, all_sends, 0)
 
     def round_trip(turn, _):
-        @pl.when(turn < BLOCKS - AHEAD)
-        def _():
-            send_step(turn + AHEAD)
-
         @pl.when(turn < BLOCKS)
         def _():
             receive(turn)
@@ -383,26 +400,15 @@
     vmem = pl.BlockSpec(memory_space=pltpu.VMEM)
     hbm = pl.BlockSpec(memory_space=pltpu.HBM)
     dma = pltpu.SemaphoreType.DMA
-    pieces = pl.pallas_call(
-        cut_kernel,
-        out_shape=jax.ShapeDtypeStruct((SEGMENTS, LANES, SEG), jnp.float32),
-        in_specs=[hbm, hbm],
+    return pl.pallas_call(
+        kernel,
+        out_shape=jax.ShapeDtypeStruct((1, LANES, LAGS), jnp.float32),
+        in_specs=[hbm] * 5,
         out_specs=vmem,
         scratch_shapes=[
             pltpu.SMEM((SEGMENTS,), jnp.int32),
-            pltpu.VMEM((SEGMENTS, LANES, CUT), jnp.float32),
-            dma,
-            dma((SEGMENTS,)),
-        ],
-        compiler_params=pltpu.CompilerParams(vmem_limit_bytes=56 << 20),
-    )(starts, records)
-    return pl.pallas_call(
-        kernel,
-        out_shape=jax.ShapeDtypeStruct((1, LANES, LAGS), jnp.float32),
-        in_specs=[hbm, vmem, hbm, hbm],
-        out_specs=vmem,
-        scratch_shapes=[
             pltpu.VMEM((PAIRS, LANES), jnp.int32),
+            pltpu.VMEM((SEGMENTS, LANES, SLOT), jnp.float32),
             pltpu.VMEM((2 * F, 3 * (SEG // 2)), jnp.bfloat16),
             pltpu.VMEM((F, 2 * F), jnp.bfloat16),
             pltpu.VMEM((DEVICES * ROWS, LANES), jnp.float32),
@@ -412,18 +418,20 @@
             pltpu.VMEM((2, 3 * LANES, (BLOCKS + 2 * REACH) * LANES), jnp.bfloat16),
             pltpu.VMEM((BLOCKS, PAIRS, 4, LANES), jnp.float32),
             pltpu.VMEM((DEVICES, 4, LANES), jnp.float32),
-            dma,
+            dma((2,)),
+            dma((SEGMENTS,)),
             dma((3,)),
             dma((3,)),
             dma((3,)),
             dma((BLOCKS,)),
             dma((BLOCKS,)),
             dma,
+            pltpu.SemaphoreType.REGULAR,
         ],
         compiler_params=pltpu.CompilerParams(
             collective_id=0, has_side_effects=True, vmem_limit_bytes=58 << 20
         ),
-    )(offsets.T, pieces, jnp.asarray(high), jnp.asarray(low))
+    )(starts, offsets.T, records, jnp.asarray(high), jnp.asarray(low))
 
 
 def solution(mesh):

time: 92.5 us -> 80.2 us (0.87); the launches traced: 91.3 us -> 80.1 us
  Pallas kernels: 89.5 us -> 78.4 us
    pallas_call x1, Pallas kernels: 85.1 us -> 78.4 us  [local(): pl.pallas_call(kernel, out_shape=jax.ShapeDtypeStruct((1, LANES, LAGS), j...]
    pallas_call x1 -> x0, Pallas kernels: 4.42 us -> none  [local(): pl.pallas_call(cut_kernel, out_shape=jax.ShapeDtypeStruct((SEGMENTS, LANE...]
where the time goes in v3:
time: 80.2 us; the launch traced here: 80.1 us
  Pallas kernels  78.4 us (98%)
  local copies, waits for them, and re-layouts  1.77 us (2%)
    pallas_call x1, Pallas kernels, local(): pl.pallas_call(kernel, out_shape=jax.ShapeDtypeStruct((1, LANES, LAGS), j...  78.4 us
    unnamed x1, local copies, waits for them, and re-layouts  1.77 us

profile of v3, /device:TPU:1, one launch (start us, length us, event | category | flops | bytes accessed | tf_op | source)
XLA Modules:
  0.0 80.1 jit_solution(5133450341597982363)
XLA Ops:
  0.0 78.4 %shard_map.55 = f32[1,128,768]{2,1,0:T(8,128)} custom-call(s32[4]{0:T(128)} %starts_hbm.1, s32[16,128]{1,0:T(8,128)} %bitcast.1, f32[128,4,2048]{2,1,0:T(4,128)} %records_ref.1, bf16[1024,512]{1,0:T(8,128)(2,1)} %constant.4.clone.high_ref, bf16[1024,512]{1,0:T(8,128)(2,1)} %constant.5.clone.low_ref), custom_call_target="tpu_custom_call" | custom-call | tf_op jit(solution)/shard_map/pallas_call | solution.py:403
  78.4 1.8 %copy.7 = f32[1,128,768]{2,1,0:T(8,128)} copy(f32[1,128,768]{2,1,0:T(8,128)} %shard_map.55) | data formatting | bytes 786432

commit v4 on v3

--- a/solution.py
+++ b/solution.py
@@ -24,6 +24,8 @@
 DEVICES = BLOCKS * INNER
 SEGMENTS = 4
 ROWS = 4 * SEGMENTS
+HALF_ROWS = ROWS // 2
+HEAD = 4
 QUARTER = F // 2
 REACH = SEP // LANES
 SPAN = 2 * REACH + 1
@@ -88,7 +90,7 @@
     half = SEG // 2
 
     def load_table(part):
-        source = (high_ref, high_ref, low_ref)[part]
+        source = (high_ref, low_ref)[part]
         return pltpu.make_async_copy(source, table_ref.at[:, pl.ds(part * half, half)], table_sems.at[part])
 
     def load_segment(segment):
@@ -100,7 +102,7 @@
     load_offsets.start()
     for segment in range(2):
         load_segment(segment).start()
-    for part in range(3):
+    for part in range(2):
         load_table(part).start()
     for segment in range(2, SEGMENTS):
         load_segment(segment).start()
@@ -119,6 +121,14 @@
         return 0
 
     lax.fori_loop(1, INNER, greet, 0)
+
+    pl.semaphore_wait(barrier, 2 * (INNER - 1))
+
+    def pass_on(step, _):
+        pl.semaphore_signal(row_sem, inc=1, device_id=peer_in_column(step), device_id_type=MESH)
+        return 0
+
+    lax.fori_loop(1, BLOCKS, pass_on, 0)
 
     load_offsets.wait()
     channel_ids = lax.broadcasted_iota(jnp.int32, (1, LANES), 1)
@@ -145,7 +155,7 @@
     window = (0.5 - 0.5 * jnp.cos(2.0 * jnp.pi / SEG * samples))[:1]
     load_starts.wait()
     lanes = lax.broadcasted_iota(jnp.int32, (LANES, LANES), 1)
-    for part in range(3):
+    for part in range(2):
         load_table(part).wait()
 
     def transform(first_segment):
@@ -171,6 +181,7 @@
             high, low = split(front + back if parity == 0 else front - back)
             stacked = jnp.concatenate([high, low, high], 1)
             rows = table_ref[pl.ds(parity * 2 * QUARTER, 2 * QUARTER), :]
+            rows = jnp.concatenate([rows[:, :half], rows], 1)
             parts.append(dot(rows, stacked, ((1,), (1,))))
         power = jnp.concatenate(
             [part[:QUARTER] * part[:QUARTER] + part[QUARTER:] * part[QUARTER:] for part in parts], 0
@@ -182,36 +193,30 @@
             for component in range(2):
                 value = parts[parity][component * QUARTER : (component + 1) * QUARTER] * part_scale
                 for second in range(2):
-                    row = (parity * 2 + component) * SEGMENTS + first_segment + second
+                    row = first_segment // 2 * HALF_ROWS + (parity * 2 + component) * 2 + second
                     send_ref[pl.ds(row, QUARTER, stride=ROWS), :] = value[:, second * LANES : (second + 1) * LANES]
 
     transform(0)
-    pl.semaphore_wait(barrier, 2 * (INNER - 1))
-
-    def pass_on(step, _):
-        pl.semaphore_signal(row_sem, inc=1, device_id=peer_in_column(step), device_id_type=MESH)
-        return 0
-
-    lax.fori_loop(1, BLOCKS, pass_on, 0)
-    transform(2)
     pl.semaphore_wait(row_sem, BLOCKS - 1)
 
     def chunk(device):
         return pl.ds(pl.multiple_of(device * ROWS, ROWS), ROWS)
 
-    own_chunk = pltpu.make_async_copy(send_ref.at[chunk(me)], recv_ref.at[chunk(me)], local_sems.at[0])
-    own_chunk.start()
-    own_place = pltpu.make_async_copy(place_ref, places_ref.at[my_block], local_sems.at[1])
-    own_place.start()
-
-    def send_step(step):
-        block = lax.rem(my_block + step, BLOCKS)
-
-        def send_one(shift, _):
-            other = lax.rem(my_inner + shift, INNER)
+    def part_of_chunk(device, first, count):
+        return pl.ds(pl.multiple_of(device * ROWS + first, HALF_ROWS), count)
+
+    def shift_of(place):
+        away = (place + 1) >> 1
+        return jnp.where((place & 1) == 1, away, INNER - away) & (INNER - 1)
+
+    def send_step(step, first, count):
+        block = (my_block + step) & (BLOCKS - 1)
+
+        def send_one(place, _):
+            other = (my_inner + shift_of(place)) & (INNER - 1)
             pltpu.make_async_remote_copy(
-                src_ref=send_ref.at[chunk(block * INNER + other)],
-                dst_ref=recv_ref.at[chunk(me)],
+                src_ref=send_ref.at[part_of_chunk(block * INNER + other, first, count)],
+                dst_ref=recv_ref.at[part_of_chunk(me, first, count)],
                 send_sem=send_sems.at[0],
                 recv_sem=recv_sems.at[step],
                 device_id=(block, other),
@@ -224,14 +229,34 @@
         @pl.when(step > 0)
         def _():
             send_one(0, 0)
-            pltpu.make_async_remote_copy(
-                src_ref=place_ref,
-                dst_ref=places_ref.at[my_block],
-                send_sem=send_sems.at[1],
-                recv_sem=place_sems.at[step],
-                device_id=(block, my_inner),
-                device_id_type=MESH,
-            ).start()
+
+    def send_places(step, _):
+        pltpu.make_async_remote_copy(
+            src_ref=place_ref,
+            dst_ref=places_ref.at[my_block],
+            send_sem=send_sems.at[1],
+            recv_sem=place_sems.at[step],
+            device_id=((my_block + step) & (BLOCKS - 1), my_inner),
+            device_id_type=MESH,
+        ).start()
+        return 0
+
+    def sends(first_step, last_step, first, count):
+        def one_step(step, _):
+            send_step(step, first, count)
+            return 0
+
+        lax.fori_loop(first_step, last_step, one_step, 0)
+
+    own_place = pltpu.make_async_copy(place_ref, places_ref.at[my_block], local_sems.at[1])
+    own_place.start()
+    sends(0, HEAD, 0, HALF_ROWS)
+    transform(2)
+    own_chunk = pltpu.make_async_copy(send_ref.at[chunk(me)], recv_ref.at[chunk(me)], local_sems.at[0])
+    own_chunk.start()
+    sends(0, HEAD, HALF_ROWS, HALF_ROWS)
+    lax.fori_loop(1, BLOCKS, send_places, 0)
+    sends(HEAD, BLOCKS, 0, ROWS)
 
     next_device = (lax.rem(my_block + 1, BLOCKS), my_inner)
 
@@ -246,14 +271,22 @@
         )
 
     block_rows = INNER * ROWS
-    flips = lax.broadcasted_iota(jnp.int32, (INNER, 2 * SEGMENTS, LANES), 1) < SEGMENTS
+    places8 = lax.broadcasted_iota(jnp.int32, (INNER, HALF_ROWS, LANES), 1)
+    lower = places8 < HALF_ROWS // 2
+    real = places8 & 2 == 0
 
     def block_of(step):
         return lax.rem(my_block + BLOCKS - step, BLOCKS)
 
     def block_values(block):
         values = recv_ref[pl.ds(pl.multiple_of(block * block_rows, block_rows), block_rows), :]
-        return values.reshape(INNER, ROWS, LANES)
+        values = values.reshape(INNER, ROWS, LANES)
+        early, late = values[:, :HALF_ROWS], values[:, HALF_ROWS:]
+        turn = HALF_ROWS // 2
+        return (
+            jnp.where(lower, early, pltpu.roll(late, turn, 1)),
+            jnp.where(lower, pltpu.roll(early, turn, 1), late),
+        )
 
     def receive(step):
         @pl.when(step == 0)
@@ -279,7 +312,7 @@
 
         values = block_values(block_of(step))
         for parity in range(2):
-            value = values[:, parity * 2 * SEGMENTS : (parity + 1) * 2 * SEGMENTS, :].reshape(LANES, LANES)
+            value = values[parity].reshape(LANES, LANES)
             high, low = split(value)
             stacked = jnp.concatenate([high, low, high], 0)
 
@@ -305,9 +338,8 @@
         picked = jnp.zeros((LANES, LANES), jnp.float32)
         columns = pl.ds(pl.multiple_of((BLOCKS - 1 - step) * LANES, LANES), SPAN * LANES)
         for parity in range(2):
-            value = values[:, parity * 2 * SEGMENTS : (parity + 1) * 2 * SEGMENTS, :]
-            turned = pltpu.roll(value, SEGMENTS, 1)
-            turned = jnp.where(flips, turned, -turned)
+            value = values[parity]
+            turned = jnp.where(real, pltpu.roll(value, HALF_ROWS - 2, 1), -pltpu.roll(value, 2, 1))
             left = jnp.concatenate([value.reshape(LANES, LANES).T, turned.reshape(LANES, LANES).T], 0)
             high, low = split(left)
             gram = dot(jnp.concatenate([high, high, low], 1), right_ref[parity, :, columns], ((1,), (0,)))
@@ -323,7 +355,7 @@
             found_ref[step, pair] = picked[4 * pair : 4 * pair + 4]
 
         def send_pair(shift, _):
-            pair = lax.rem(my_inner + shift, INNER)
+            pair = (my_inner + shift_of(shift)) & (INNER - 1)
             pltpu.make_async_remote_copy(
                 src_ref=found_ref.at[step, pair],
                 dst_ref=cross_ref.at[me],
@@ -340,12 +372,6 @@
         def _():
             send_pair(0, 0)
 
-    def all_sends(step, _):
-        send_step(step)
-        return 0
-
-    lax.fori_loop(0, BLOCKS, all_sends, 0)
-
     def round_trip(turn, _):
         @pl.when(turn < BLOCKS)
         def _():
@@ -373,7 +399,7 @@
             place = parity * 2 + component
             high, low = split(cross_ref[:, place, :])
             rows = table_ref[pl.ds(place * QUARTER, QUARTER), :]
-            table_high, table_low = rows[:, :half], rows[:, 2 * half :]
+            table_high, table_low = rows[:, :half], rows[:, half:]
             first = ((0,), (0,))
             term = dot(high, table_high, first) + (dot(high, table_low, first) + dot(low, table_high, first))
             total = term if total is None else total + term
@@ -400,6 +426,7 @@
     vmem = pl.BlockSpec(memory_space=pltpu.VMEM)
     hbm = pl.BlockSpec(memory_space=pltpu.HBM)
     dma = pltpu.SemaphoreType.DMA
+    operands = (starts, offsets.T, records, jnp.asarray(high), jnp.asarray(low))
     return pl.pallas_call(
         kernel,
         out_shape=jax.ShapeDtypeStruct((1, LANES, LAGS), jnp.float32),
@@ -409,7 +436,7 @@
             pltpu.SMEM((SEGMENTS,), jnp.int32),
             pltpu.VMEM((PAIRS, LANES), jnp.int32),
             pltpu.VMEM((SEGMENTS, LANES, SLOT), jnp.float32),
-            pltpu.VMEM((2 * F, 3 * (SEG // 2)), jnp.bfloat16),
+            pltpu.VMEM((2 * F, SEG), jnp.bfloat16),
             pltpu.VMEM((F, 2 * F), jnp.bfloat16),
             pltpu.VMEM((DEVICES * ROWS, LANES), jnp.float32),
             pltpu.VMEM((DEVICES * ROWS, LANES), jnp.float32),
@@ -420,7 +447,7 @@
             pltpu.VMEM((DEVICES, 4, LANES), jnp.float32),
             dma((2,)),
             dma((SEGMENTS,)),
-            dma((3,)),
+            dma((2,)),
             dma((3,)),
             dma((3,)),
             dma((BLOCKS,)),
@@ -429,9 +456,9 @@
             pltpu.SemaphoreType.REGULAR,
         ],
         compiler_params=pltpu.CompilerParams(
-            collective_id=0, has_side_effects=True, vmem_limit_bytes=58 << 20
+            collective_id=0, has_side_effects=True, vmem_limit_bytes=48 << 20
         ),
-    )(starts, offsets.T, records, jnp.asarray(high), jnp.asarray(low))
+    )(*(pltpu.with_memory_space_constraint(value, pltpu.HBM) for value in operands))
 
 
 def solution(mesh):

time: 80.2 us -> 78 us (0.973)
  Pallas kernels: 78.4 us -> 77.1 us
  local copies, waits for them, and re-layouts: 1.77 us -> 0.75 us
    pallas_call x1, Pallas kernels: 78.4 us -> 77.1 us  [local(): pl.pallas_call(kernel, out_shape=jax.ShapeDtypeStruct((1, LANES, LAGS), j...]
    unnamed x1, local copies, waits for them, and re-layouts: 1.77 us -> 0.75 us
where the time goes in v4:
time: 78 us; the launch traced here: 77.9 us
  Pallas kernels  77.1 us (99%)
    pallas_call x1, Pallas kernels, local(): pl.pallas_call(kernel, out_shape=jax.ShapeDtypeStruct((1, LANES, LAGS), j...  77.1 us

profile of v4, /device:TPU:1, one launch (start us, length us, event | category | flops | bytes accessed | tf_op | source)
XLA Modules:
  0.0 77.9 jit_solution(13040274219927671388)
XLA Ops:
  0.0 77.1 %shard_map.55 = f32[1,128,768]{2,1,0:T(8,128)S(1)} custom-call(s32[4]{0:T(128)} %starts_hbm.1, s32[16,128]{1,0:T(8,128)} %bitcast.1, f32[128,4,2048]{2,1,0:T(4,128)} %records_ref.1, bf16[1024,512]{1,0:T(8,128)(2,1)} %constant.4.clone.high_ref, bf16[1024,512]{1,0:T(8,128)(2,1)} %constant.5.clone.low_ref), custom_call_target="tpu_custom_call" | custom-call | tf_op jit(solution)/shard_map/pallas_call | solution.py:430
  77.1 0.7 copy.7

commit v5 on v4

--- a/solution.py
+++ b/solution.py
@@ -24,7 +24,13 @@
 DEVICES = BLOCKS * INNER
 SEGMENTS = 4
 ROWS = 4 * SEGMENTS
-HALF_ROWS = ROWS // 2
+PLANES = 8
+OWNERS = DEVICES // 2
+OWNED = 4
+TILE = 2 * SEGMENTS
+CHUNK = OWNED * TILE
+BLOCK_ROWS = 8 * CHUNK
+PARTS = 2 * OWNED
 HEAD = 4
 QUARTER = F // 2
 REACH = SEP // LANES
@@ -36,7 +42,8 @@
     samples = np.arange(SEG // 2, dtype=np.int64)
     rows = []
     for parity in range(2):
-        bins = 2 * np.arange(QUARTER, dtype=np.int64) + parity
+        order = np.arange(QUARTER, dtype=np.int64)
+        bins = 2 * (order % OWNERS * 2 + order // OWNERS) + parity
         angle = 2.0 * np.pi / SEG * (bins[:, None] * samples[None, :] % SEG)
         rows += [np.cos(angle), -np.sin(angle)]
     table = np.concatenate(rows, 0).astype(np.float32)
@@ -69,7 +76,6 @@
     band_ref,
     send_ref,
     recv_ref,
-    place_ref,
     places_ref,
     right_ref,
     found_ref,
@@ -131,14 +137,11 @@
     lax.fori_loop(1, BLOCKS, pass_on, 0)
 
     load_offsets.wait()
-    channel_ids = lax.broadcasted_iota(jnp.int32, (1, LANES), 1)
-    for pair in range(PAIRS):
-        row = offsets_ref[pl.ds(pair, 1), :] + (channel_ids + SEP)
-        place_ref[pl.ds(4 * pair, 4), :] = jnp.broadcast_to(row, (4, LANES))
-
-    gap = 2 * (
-        lax.broadcasted_iota(jnp.int32, (QUARTER, QUARTER), 0) - lax.broadcasted_iota(jnp.int32, (QUARTER, QUARTER), 1)
-    )
+    def number(axis):
+        order = lax.broadcasted_iota(jnp.int32, (QUARTER, QUARTER), axis)
+        return ((order & (OWNERS - 1)) << 1) + (order >> 7)
+
+    gap = 2 * (number(0) - number(1))
 
     def near_bins(shift):
         distance = jnp.abs(gap + shift)
@@ -155,6 +158,7 @@
     window = (0.5 - 0.5 * jnp.cos(2.0 * jnp.pi / SEG * samples))[:1]
     load_starts.wait()
     lanes = lax.broadcasted_iota(jnp.int32, (LANES, LANES), 1)
+    channel_ids = lax.broadcasted_iota(jnp.int32, (LANES, LANES), 0)
     for part in range(2):
         load_table(part).wait()
 
@@ -193,46 +197,65 @@
             for component in range(2):
                 value = parts[parity][component * QUARTER : (component + 1) * QUARTER] * part_scale
                 for second in range(2):
-                    row = first_segment // 2 * HALF_ROWS + (parity * 2 + component) * 2 + second
-                    send_ref[pl.ds(row, QUARTER, stride=ROWS), :] = value[:, second * LANES : (second + 1) * LANES]
+                    for which in range(2):
+                        row = (which * 2 + 1 - parity) * TILE + component * SEGMENTS + first_segment + second
+                        send_ref[pl.ds(row, OWNERS, stride=CHUNK), :] = value[
+                            which * OWNERS : (which + 1) * OWNERS, second * LANES : (second + 1) * LANES
+                        ]
 
     transform(0)
+    transform(2)
     pl.semaphore_wait(row_sem, BLOCKS - 1)
 
-    def chunk(device):
-        return pl.ds(pl.multiple_of(device * ROWS, ROWS), ROWS)
-
-    def part_of_chunk(device, first, count):
-        return pl.ds(pl.multiple_of(device * ROWS + first, HALF_ROWS), count)
+    my_plane = my_inner & (PLANES - 1)
+    my_side = my_inner >> 3
+
+    def owner_of(block, side, plane):
+        return (plane & 3) * (2 * BLOCKS) + block * 2 + side
+
+    def send_rows(block, side, plane, first, count):
+        return send_ref.at[pl.ds(pl.multiple_of(owner_of(block, side, plane) * CHUNK + first, TILE), count)]
+
+    def recv_rows(slot, first, count):
+        start = my_block * BLOCK_ROWS + (slot * 2 + my_side) * CHUNK + first
+        return recv_ref.at[pl.ds(pl.multiple_of(start, TILE), count)]
+
+    def send_step(step, _):
+        block = (my_block + step) & (BLOCKS - 1)
+        for turn in range(2):
+            side = my_side ^ turn
+            for ahead in (1, -1, 2, -2, 0):
+                plane = (my_plane + ahead) & (PLANES - 1)
+                if abs(ahead) < 2:
+                    pieces = [(1 - ahead, 0, CHUNK)]
+                else:
+                    parity_row = 0 if ahead == 2 else TILE
+                    pieces = [(3, parity_row, TILE), (3, parity_row + 2 * TILE, TILE)]
+
+                def go():
+                    for slot, first, count in pieces:
+                        pltpu.make_async_remote_copy(
+                            src_ref=send_rows(block, side, plane, first, count),
+                            dst_ref=recv_rows(slot, first, count),
+                            send_sem=send_sems.at[0],
+                            recv_sem=recv_sems.at[step],
+                            device_id=(block, side * PLANES + plane),
+                            device_id_type=MESH,
+                        ).start()
+
+                if turn == 0 and ahead == 0:
+                    pl.when(step > 0)(go)
+                else:
+                    go()
+        return 0
 
     def shift_of(place):
         away = (place + 1) >> 1
         return jnp.where((place & 1) == 1, away, INNER - away) & (INNER - 1)
 
-    def send_step(step, first, count):
-        block = (my_block + step) & (BLOCKS - 1)
-
-        def send_one(place, _):
-            other = (my_inner + shift_of(place)) & (INNER - 1)
-            pltpu.make_async_remote_copy(
-                src_ref=send_ref.at[part_of_chunk(block * INNER + other, first, count)],
-                dst_ref=recv_ref.at[part_of_chunk(me, first, count)],
-                send_sem=send_sems.at[0],
-                recv_sem=recv_sems.at[step],
-                device_id=(block, other),
-                device_id_type=MESH,
-            ).start()
-            return 0
-
-        lax.fori_loop(1, INNER, send_one, 0)
-
-        @pl.when(step > 0)
-        def _():
-            send_one(0, 0)
-
     def send_places(step, _):
         pltpu.make_async_remote_copy(
-            src_ref=place_ref,
+            src_ref=offsets_ref,
             dst_ref=places_ref.at[my_block],
             send_sem=send_sems.at[1],
             recv_sem=place_sems.at[step],
@@ -241,22 +264,15 @@
         ).start()
         return 0
 
-    def sends(first_step, last_step, first, count):
-        def one_step(step, _):
-            send_step(step, first, count)
-            return 0
-
-        lax.fori_loop(first_step, last_step, one_step, 0)
-
-    own_place = pltpu.make_async_copy(place_ref, places_ref.at[my_block], local_sems.at[1])
+    own_place = pltpu.make_async_copy(offsets_ref, places_ref.at[my_block], local_sems.at[1])
     own_place.start()
-    sends(0, HEAD, 0, HALF_ROWS)
-    transform(2)
-    own_chunk = pltpu.make_async_copy(send_ref.at[chunk(me)], recv_ref.at[chunk(me)], local_sems.at[0])
+    own_chunk = pltpu.make_async_copy(
+        send_rows(my_block, my_side, my_plane, 0, CHUNK), recv_rows(1, 0, CHUNK), local_sems.at[0]
+    )
     own_chunk.start()
-    sends(0, HEAD, HALF_ROWS, HALF_ROWS)
+    lax.fori_loop(0, HEAD, send_step, 0)
     lax.fori_loop(1, BLOCKS, send_places, 0)
-    sends(HEAD, BLOCKS, 0, ROWS)
+    lax.fori_loop(HEAD, BLOCKS, send_step, 0)
 
     next_device = (lax.rem(my_block + 1, BLOCKS), my_inner)
 
@@ -270,23 +286,19 @@
             device_id_type=MESH,
         )
 
-    block_rows = INNER * ROWS
-    places8 = lax.broadcasted_iota(jnp.int32, (INNER, HALF_ROWS, LANES), 1)
-    lower = places8 < HALF_ROWS // 2
-    real = places8 & 2 == 0
+    real = lax.broadcasted_iota(jnp.int32, (TILE, TILE, LANES), 1) < SEGMENTS
 
     def block_of(step):
         return lax.rem(my_block + BLOCKS - step, BLOCKS)
 
     def block_values(block):
-        values = recv_ref[pl.ds(pl.multiple_of(block * block_rows, block_rows), block_rows), :]
-        values = values.reshape(INNER, ROWS, LANES)
-        early, late = values[:, :HALF_ROWS], values[:, HALF_ROWS:]
-        turn = HALF_ROWS // 2
-        return (
-            jnp.where(lower, early, pltpu.roll(late, turn, 1)),
-            jnp.where(lower, pltpu.roll(early, turn, 1), late),
-        )
+        values = recv_ref[pl.ds(pl.multiple_of(block * BLOCK_ROWS, BLOCK_ROWS), BLOCK_ROWS), :]
+        return values.reshape(8, OWNED, TILE, LANES)
+
+    def parts_of(value):
+        flat = value.reshape(8 * TILE, LANES)
+        high = flat.astype(jnp.bfloat16).astype(jnp.float32)
+        return high, flat - high
 
     def receive(step):
         @pl.when(step == 0)
@@ -294,8 +306,8 @@
             own_chunk.wait()
             own_place.wait()
             awaited(
-                send_ref.at[pl.ds(0, block_rows - ROWS)],
-                recv_ref.at[pl.ds(0, block_rows - ROWS)],
+                send_ref.at[pl.ds(0, BLOCK_ROWS - CHUNK)],
+                recv_ref.at[pl.ds(0, BLOCK_ROWS - CHUNK)],
                 send_sems.at[0],
                 recv_sems.at[0],
             ).wait_recv()
@@ -303,21 +315,20 @@
         @pl.when(step > 0)
         def _():
             awaited(
-                send_ref.at[pl.ds(0, block_rows)],
-                recv_ref.at[pl.ds(0, block_rows)],
+                send_ref.at[pl.ds(0, BLOCK_ROWS)],
+                recv_ref.at[pl.ds(0, BLOCK_ROWS)],
                 send_sems.at[0],
                 recv_sems.at[step],
             ).wait_recv()
-            awaited(place_ref, places_ref.at[0], send_sems.at[1], place_sems.at[step]).wait_recv()
+            awaited(offsets_ref, places_ref.at[0], send_sems.at[1], place_sems.at[step]).wait_recv()
 
         values = block_values(block_of(step))
-        for parity in range(2):
-            value = values[parity].reshape(LANES, LANES)
-            high, low = split(value)
-            stacked = jnp.concatenate([high, low, high], 0)
+        for which in range(OWNED):
+            high, low = parts_of(values[:, which])
+            stacked = jnp.concatenate([high, high, low, low], 0).astype(jnp.bfloat16)
 
             def place_at(slot):
-                right_ref[parity, :, pl.ds(pl.multiple_of(slot * LANES, LANES), LANES)] = stacked
+                right_ref[which, :, pl.ds(pl.multiple_of(slot * LANES, LANES), LANES)] = stacked
 
             place_at(BLOCKS + 1 - step)
 
@@ -329,36 +340,45 @@
             def _():
                 place_at(BLOCKS + 1 - step + BLOCKS)
 
+    def found_rows(step, pair):
+        return found_ref.at[step, pl.ds(pl.multiple_of(pair * PARTS, PARTS), PARTS)]
+
+    my_slot = (my_plane >> 2) * OWNERS + owner_of(my_block, my_side, my_plane)
+    cross_rows = cross_ref.at[pl.ds(pl.multiple_of(my_slot * PARTS, PARTS), PARTS)]
+
     def correlate(step):
         block = block_of(step)
         values = block_values(block)
-        place = jnp.concatenate([places_ref[block], jnp.zeros((LANES - 4 * PAIRS, LANES), jnp.int32)], 0).T
-        lane = place % LANES
-        code = place // LANES * 4 + lanes % 4
+        offsets = places_ref[block]
+        place = jnp.concatenate(
+            [jnp.broadcast_to(offsets[pair : pair + 1], (PARTS, LANES)) for pair in range(PAIRS)], 0
+        ).T + (channel_ids + SEP)
+        lane = place & (LANES - 1)
+        code = (place >> 7) * PARTS + (lanes & (PARTS - 1))
         picked = jnp.zeros((LANES, LANES), jnp.float32)
         columns = pl.ds(pl.multiple_of((BLOCKS - 1 - step) * LANES, LANES), SPAN * LANES)
-        for parity in range(2):
-            value = values[parity]
-            turned = jnp.where(real, pltpu.roll(value, HALF_ROWS - 2, 1), -pltpu.roll(value, 2, 1))
-            left = jnp.concatenate([value.reshape(LANES, LANES).T, turned.reshape(LANES, LANES).T], 0)
-            high, low = split(left)
-            gram = dot(jnp.concatenate([high, high, low], 1), right_ref[parity, :, columns], ((1,), (0,)))
+        for which in range(OWNED):
+            value = values[:, which]
+            turned = pltpu.roll(value, SEGMENTS, 1)
+            turned = jnp.where(real, turned, -turned)
+            left = jnp.concatenate(
+                [jnp.concatenate(parts_of(kind), 0).T.astype(jnp.bfloat16) for kind in (value, turned)], 0
+            )
+            gram = dot(jnp.concatenate([left, left], 1), right_ref[which, :, columns], ((1,), (0,)))
             for component in range(2):
                 for near in range(SPAN):
                     tile = gram[
                         component * LANES : (component + 1) * LANES, near * LANES : (near + 1) * LANES
                     ]
                     value_there = jnp.take_along_axis(tile, lane, axis=1, mode="promise_in_bounds")
-                    picked = jnp.where(code == near * 4 + parity * 2 + component, value_there, picked)
-        picked = picked.T
-        for pair in range(PAIRS):
-            found_ref[step, pair] = picked[4 * pair : 4 * pair + 4]
+                    picked = jnp.where(code == near * PARTS + which * 2 + component, value_there, picked)
+        found_ref[step] = picked.T
 
         def send_pair(shift, _):
             pair = (my_inner + shift_of(shift)) & (INNER - 1)
             pltpu.make_async_remote_copy(
-                src_ref=found_ref.at[step, pair],
-                dst_ref=cross_ref.at[me],
+                src_ref=found_rows(step, pair),
+                dst_ref=cross_rows,
                 send_sem=send_sems.at[2],
                 recv_sem=cross_sem,
                 device_id=(block, pair),
@@ -385,25 +405,30 @@
 
     lax.fori_loop(0, BLOCKS + 2 * REACH, round_trip, 0)
 
-    own_cross = pltpu.make_async_copy(found_ref.at[0, my_inner], cross_ref.at[me], local_sems.at[2])
+    own_cross = pltpu.make_async_copy(found_rows(0, my_inner), cross_rows, local_sems.at[2])
     own_cross.start()
     own_cross.wait()
     awaited(
-        cross_ref.at[pl.ds(0, DEVICES - 1)], cross_ref.at[pl.ds(0, DEVICES - 1)], send_sems.at[2], cross_sem
+        cross_ref.at[pl.ds(0, (DEVICES - 1) * PARTS)], cross_ref.at[pl.ds(0, (DEVICES - 1) * PARTS)], send_sems.at[2], cross_sem
     ).wait_recv()
+
+    def summed(parity, component, which):
+        part = (which * 2 + 1 - parity) * 2 + component
+        return (
+            cross_ref[pl.ds(part, OWNERS, stride=PARTS), :]
+            + cross_ref[pl.ds(OWNERS * PARTS + part, OWNERS, stride=PARTS), :]
+        )
 
     sums = []
     for parity in range(2):
-        total = None
-        for component in range(2):
-            place = parity * 2 + component
-            high, low = split(cross_ref[:, place, :])
-            rows = table_ref[pl.ds(place * QUARTER, QUARTER), :]
-            table_high, table_low = rows[:, :half], rows[:, half:]
-            first = ((0,), (0,))
-            term = dot(high, table_high, first) + (dot(high, table_low, first) + dot(low, table_high, first))
-            total = term if total is None else total + term
-        sums.append(total)
+        spectrum = jnp.concatenate(
+            [summed(parity, component, which) for component in range(2) for which in range(2)], 0
+        )
+        high, low = split(spectrum)
+        rows = table_ref[pl.ds(parity * 2 * QUARTER, 2 * QUARTER), :]
+        table_high, table_low = rows[:, :half], rows[:, half:]
+        first = ((0,), (0,))
+        sums.append(dot(high, table_high, first) + (dot(high, table_low, first) + dot(low, table_high, first)))
     even, odd = sums
     shift = LAGS // 2
     segment_count = INNER * SEGMENTS
@@ -411,13 +436,13 @@
     out_ref[0, :, pl.ds(0, shift)] = (even - odd)[:, half - shift :] * factor
     out_ref[0, :, pl.ds(shift, shift)] = (even + odd)[:, :shift] * factor
 
-    rest = DEVICES * ROWS - ROWS
+    rest = DEVICES * ROWS - CHUNK
     awaited(send_ref.at[pl.ds(0, rest)], recv_ref.at[pl.ds(0, rest)], send_sems.at[0], recv_sems.at[0]).wait_send()
     awaited(
         places_ref.at[pl.ds(0, BLOCKS - 1)], places_ref.at[pl.ds(0, BLOCKS - 1)], send_sems.at[1], place_sems.at[0]
     ).wait_send()
     awaited(
-        cross_ref.at[pl.ds(0, DEVICES - 1)], cross_ref.at[pl.ds(0, DEVICES - 1)], send_sems.at[2], cross_sem
+        cross_ref.at[pl.ds(0, (DEVICES - 1) * PARTS)], cross_ref.at[pl.ds(0, (DEVICES - 1) * PARTS)], send_sems.at[2], cross_sem
     ).wait_send()
 
 
@@ -440,11 +465,10 @@
             pltpu.VMEM((F, 2 * F), jnp.bfloat16),
             pltpu.VMEM((DEVICES * ROWS, LANES), jnp.float32),
             pltpu.VMEM((DEVICES * ROWS, LANES), jnp.float32),
-            pltpu.VMEM((4 * PAIRS, LANES), jnp.int32),
-            pltpu.VMEM((BLOCKS, 4 * PAIRS, LANES), jnp.int32),
-            pltpu.VMEM((2, 3 * LANES, (BLOCKS + 2 * REACH) * LANES), jnp.bfloat16),
-            pltpu.VMEM((BLOCKS, PAIRS, 4, LANES), jnp.float32),
-            pltpu.VMEM((DEVICES, 4, LANES), jnp.float32),
+            pltpu.VMEM((BLOCKS, PAIRS, LANES), jnp.int32),
+            pltpu.VMEM((OWNED, 2 * LANES, (BLOCKS + 2 * REACH) * LANES), jnp.bfloat16),
+            pltpu.VMEM((BLOCKS, PAIRS * PARTS, LANES), jnp.float32),
+            pltpu.VMEM((DEVICES * PARTS, LANES), jnp.float32),
             dma((2,)),
             dma((SEGMENTS,)),
             dma((2,)),

time: 78 us -> 90.5 us (1.16)
  Pallas kernels: 77.1 us -> 89.5 us
    pallas_call x1, Pallas kernels: 77.1 us -> 89.5 us  [local(): pl.pallas_call(kernel, out_shape=jax.ShapeDtypeStruct((1, LANES, LAGS), j...]
where the time goes in v5:
time: 90.5 us; the launch traced here: 90.3 us
  Pallas kernels  89.5 us (99%)
    pallas_call x1, Pallas kernels, local(): pl.pallas_call(kernel, out_shape=jax.ShapeDtypeStruct((1, LANES, LAGS), j...  89.5 us

profile of v5, /device:TPU:1, one launch (start us, length us, event | category | flops | bytes accessed | tf_op | source)
XLA Modules:
  0.0 90.3 jit_solution(7717572734903943231)
XLA Ops:
  0.0 89.5 %shard_map.55 = f32[1,128,768]{2,1,0:T(8,128)S(1)} custom-call(s32[4]{0:T(128)} %starts_hbm.1, s32[16,128]{1,0:T(8,128)} %bitcast.1, f32[128,4,2048]{2,1,0:T(4,128)} %records_ref.1, bf16[1024,512]{1,0:T(8,128)(2,1)} %constant.4.clone.high_ref, bf16[1024,512]{1,0:T(8,128)(2,1)} %constant.5.clone.low_ref), custom_call_target="tpu_custom_call" | custom-call | tf_op jit(solution)/shard_map/pallas_call | solution.py:455
  89.6 0.7 copy.7

commit v6 on v4

--- a/solution.py
+++ b/solution.py
@@ -26,6 +26,7 @@
 ROWS = 4 * SEGMENTS
 HALF_ROWS = ROWS // 2
 HEAD = 4
+UNROLL = 16
 QUARTER = F // 2
 REACH = SEP // LANES
 SPAN = 2 * REACH + 1
@@ -74,6 +75,9 @@
     right_ref,
     found_ref,
     cross_ref,
+    index_ref,
+    gram_ref,
+    picked_ref,
     index_sems,
     load_sems,
     table_sems,
@@ -333,24 +337,36 @@
         block = block_of(step)
         values = block_values(block)
         place = jnp.concatenate([places_ref[block], jnp.zeros((LANES - 4 * PAIRS, LANES), jnp.int32)], 0).T
-        lane = place % LANES
-        code = place // LANES * 4 + lanes % 4
-        picked = jnp.zeros((LANES, LANES), jnp.float32)
+        index_ref[...] = place
         columns = pl.ds(pl.multiple_of((BLOCKS - 1 - step) * LANES, LANES), SPAN * LANES)
         for parity in range(2):
             value = values[parity]
             turned = jnp.where(real, pltpu.roll(value, HALF_ROWS - 2, 1), -pltpu.roll(value, 2, 1))
             left = jnp.concatenate([value.reshape(LANES, LANES).T, turned.reshape(LANES, LANES).T], 0)
             high, low = split(left)
-            gram = dot(jnp.concatenate([high, high, low], 1), right_ref[parity, :, columns], ((1,), (0,)))
-            for component in range(2):
+            gram_ref[pl.ds(parity * 2 * LANES, 2 * LANES), :] = dot(
+                jnp.concatenate([high, high, low], 1), right_ref[parity, :, columns], ((1,), (0,))
+            )
+        part_lanes = lanes[:8] & 3
+
+        def pick(group, _):
+            rows = pl.ds(pl.multiple_of(group * 8, 8), 8)
+            place = index_ref[rows, :]
+            lane = place & (LANES - 1)
+            code = (place >> 7) * 4 + part_lanes
+            picked = jnp.zeros((8, LANES), jnp.float32)
+            for part in range(4):
                 for near in range(SPAN):
-                    tile = gram[
-                        component * LANES : (component + 1) * LANES, near * LANES : (near + 1) * LANES
-                    ]
-                    value_there = jnp.take_along_axis(tile, lane, axis=1, mode="promise_in_bounds")
-                    picked = jnp.where(code == near * 4 + parity * 2 + component, value_there, picked)
-        picked = picked.T
+                    source = pl.ds(pl.multiple_of(part * LANES + group * 8, 8), 8)
+                    value_there = jnp.take_along_axis(
+                        gram_ref[source, pl.ds(near * LANES, LANES)], lane, axis=1, mode="promise_in_bounds"
+                    )
+                    picked = jnp.where(code == near * 4 + part, value_there, picked)
+            picked_ref[rows, :] = picked
+            return 0
+
+        lax.fori_loop(0, LANES // 8, pick, 0, unroll=UNROLL)
+        picked = picked_ref[...].T
         for pair in range(PAIRS):
             found_ref[step, pair] = picked[4 * pair : 4 * pair + 4]
 
@@ -394,16 +410,17 @@
 
     sums = []
     for parity in range(2):
-        total = None
-        for component in range(2):
-            place = parity * 2 + component
-            high, low = split(cross_ref[:, place, :])
-            rows = table_ref[pl.ds(place * QUARTER, QUARTER), :]
-            table_high, table_low = rows[:, :half], rows[:, half:]
-            first = ((0,), (0,))
-            term = dot(high, table_high, first) + (dot(high, table_low, first) + dot(low, table_high, first))
-            total = term if total is None else total + term
-        sums.append(total)
+        spectrum = jnp.concatenate([cross_ref[:, parity * 2 + component, :] for component in range(2)], 0)
+        high, low = split(spectrum)
+        rows = table_ref[pl.ds(parity * 2 * QUARTER, 2 * QUARTER), :]
+        table_high, table_low = rows[:, :half], rows[:, half:]
+        sums.append(
+            dot(
+                jnp.concatenate([high, high, low], 0),
+                jnp.concatenate([table_high, table_low, table_high], 0),
+                ((0,), (0,)),
+            )
+        )
     even, odd = sums
     shift = LAGS // 2
     segment_count = INNER * SEGMENTS
@@ -445,6 +462,9 @@
             pltpu.VMEM((2, 3 * LANES, (BLOCKS + 2 * REACH) * LANES), jnp.bfloat16),
             pltpu.VMEM((BLOCKS, PAIRS, 4, LANES), jnp.float32),
             pltpu.VMEM((DEVICES, 4, LANES), jnp.float32),
+            pltpu.VMEM((LANES, LANES), jnp.int32),
+            pltpu.VMEM((4 * LANES, SPAN * LANES), jnp.float32),
+            pltpu.VMEM((LANES, LANES), jnp.float32),
             dma((2,)),
             dma((SEGMENTS,)),
             dma((2,)),

time: 78 us -> 76.6 us (0.982)
  Pallas kernels: 77.1 us -> 75.8 us
    pallas_call x1, Pallas kernels: 77.1 us -> 75.8 us  [local(): pl.pallas_call(kernel, out_shape=jax.ShapeDtypeStruct((1, LANES, LAGS), j...]
where the time goes in v6:
time: 76.6 us
  Pallas kernels  75.8 us (99%)
    pallas_call x1, Pallas kernels, local(): pl.pallas_call(kernel, out_shape=jax.ShapeDtypeStruct((1, LANES, LAGS), j...  75.8 us

profile of v6, /device:TPU:1, one launch (start us, length us, event | category | flops | bytes accessed | tf_op | source)
XLA Modules:
  0.0 76.6 jit_solution(13979522856550706805)
XLA Ops:
  0.0 75.8 %shard_map.55 = f32[1,128,768]{2,1,0:T(8,128)S(1)} custom-call(s32[4]{0:T(128)} %starts_hbm.1, s32[16,128]{1,0:T(8,128)} %bitcast.1, f32[128,4,2048]{2,1,0:T(4,128)} %records_ref.1, bf16[1024,512]{1,0:T(8,128)(2,1)} %constant.4.clone.high_ref, bf16[1024,512]{1,0:T(8,128)(2,1)} %constant.5.clone.low_ref), custom_call_target="tpu_custom_call" | custom-call | tf_op jit(solution)/shard_map/pallas_call | solution.py:447
  75.8 0.7 copy.7
